TPU v7x, 32 devices: a whole 2x2x4 slice. The times are simulated.
32 devices in a mesh: grp: 4 (over y, x), seq: 8 (over z, core).
Axes of the slice: x: 2, y: 2, z: 4, core: 2. Of those that a mesh axis runs over, the one named last changes fastest.
Arguments:
- query_proj: bfloat16 [4096, 2048], P(('grp', 'seq')), may hold values from -6 to 6
- key_proj: bfloat16 [4096, 2048], P(('grp', 'seq')), may hold values from -13 to 13
- value_proj: bfloat16 [4096, 2048], P(('grp', 'seq')), may hold values from -6 to 6
- log_decay: float32 [4096, 16], P(('grp', 'seq')), may hold values from -1 to 0, as said below
- write_rate: float32 [4096, 16], P(('grp', 'seq')), may hold values from 0 to 1, as said below
- gate_proj: bfloat16 [4096, 2048], P(('grp', 'seq')), may hold values from -6 to 6
- norm_gain: float32 [128], replicated, may hold values from 0.1 to 1.9
- initial_state: float32 [16, 128, 128], replicated, may hold values from -0.125 to 0.125
Outputs:
- mixed: bfloat16 [4096, 2048], P(('grp', 'seq'))
Inputs may be any that keep to these rules, and one draw needn't show every extreme that they name: log_decay is the logarithm of a factor in (0, 1]. write_rate is a strength in (0, 1).
All inputs are finite; a program needn't handle non-finite values.
Results may differ from a plain program's by a relative error of at most 0.0011.
Values sent between devices are 32-bit elements; how exact they have to be, the bound alone decides.
No kernel may reach another device: no remote copies, remote signals or barrier semaphores. Data moves between devices by JAX's collectives and lax.ppermute only.
A program may use at most 320 MiB of HBM per device.

v0:
```python
import jax
import jax.numpy as jnp
from jax import lax
from jax.sharding import PartitionSpec as P

ATTENTION_UNITS = 16
DK = 128
DV = 128
BLOCK = 64


HIGHEST = lax.Precision.HIGHEST


def prefix_2(x, axis, combine, identity):
    peers, place = (lax.axis_size(axis), lax.axis_index(axis))
    everything = jax.tree.map(lambda part: lax.all_gather(part, axis), x)
    start = jax.tree.map(
        lambda part, zero: jnp.broadcast_to(jnp.asarray(zero, part.dtype), part.shape), x, identity
    )

    def lap(k, before):
        reached = k < place
        new = combine(before, jax.tree.map(lambda part: part[k], everything))
        return jax.tree.map(lambda a, b: jnp.where(reached, a, b), new, before)

    return lax.fori_loop(0, peers, lap, start)


def spread_2(x, axis, root):
    mine = lax.axis_index(axis) == root
    return lax.psum(jnp.where(mine, x, jnp.zeros_like(x)), axis)


def unit_rows(entries):
    return entries * lax.rsqrt(jnp.sum(entries * entries, axis=-1, keepdims=True) + 1e-06)


def matmul(left, right):
    return jnp.einsum("...ij,...jk->...ik", left, right, precision=HIGHEST)


def inner_rows(left, right):
    return jnp.einsum("...ik,...jk->...ij", left, right, precision=HIGHEST)


def left_contract(left, right):
    return jnp.einsum("...ci,...cj->...ij", left, right, precision=HIGHEST)


def block_terms(queries, key_rows, values, decays, write_rates):
    cumulative = jnp.cumsum(decays, axis=-1)
    block_size = decays.shape[-1]
    later = lax.broadcasted_iota(jnp.int32, (block_size, block_size), 0)
    earlier = lax.broadcasted_iota(jnp.int32, (block_size, block_size), 1)
    within = later >= earlier
    before = later > earlier
    spread = cumulative[..., :, None] - cumulative[..., None, :]
    damping = jnp.where(within, jnp.exp(jnp.where(within, spread, 0.0)), 0.0)
    key_products = inner_rows(key_rows, key_rows)
    strict_part = jnp.where(before, write_rates[..., :, None] * key_products * damping, 0.0)
    unit_lower = jnp.eye(block_size, dtype=jnp.float32) + strict_part
    scaled_keys = (write_rates * jnp.exp(cumulative))[..., None] * key_rows
    scaled_values = write_rates[..., None] * values
    stacked = jnp.concatenate([scaled_keys, scaled_values], axis=-1)
    solved = lax.linalg.triangular_solve(
        unit_lower, stacked, left_side=True, lower=True, unit_diagonal=True
    )
    key_width = key_rows.shape[-1]
    erase = solved[..., :key_width]
    insert = solved[..., key_width:]
    final_log = cumulative[..., -1:]
    carried_keys = jnp.exp(final_log - cumulative)[..., None] * key_rows
    readout_mix = inner_rows(queries, key_rows) * damping
    query_scaled = jnp.exp(cumulative)[..., None] * queries
    retention = jnp.exp(final_log)[..., None]
    return (erase, insert, carried_keys, readout_mix, query_scaled, retention)


def block_apply(terms, state):
    erase, insert, carried_keys, readout_mix, query_scaled, retention = terms
    fresh_rows = insert - matmul(erase, state)
    readout = matmul(query_scaled, state) + matmul(readout_mix, fresh_rows)
    next_state = retention * state + left_contract(carried_keys, fresh_rows)
    return (readout, next_state)


def gated_norm(readout, gate, gain):
    scaled = readout * lax.rsqrt(jnp.mean(readout * readout, axis=-1, keepdims=True) + 1e-05) * gain
    return (scaled * jax.nn.silu(gate.astype(jnp.float32))).astype(jnp.bfloat16)


def compose(earlier_map, later_map):
    return (
        matmul(later_map[0], earlier_map[0]),
        matmul(later_map[0], earlier_map[1]) + later_map[1],
    )


def apply_map(state_map, state):
    return matmul(state_map[0], state) + state_map[1]


def body(
    query_proj, key_proj, value_proj, log_decay, write_rate, gate_proj, norm_gain, initial_state
):
    length = query_proj.shape[0]
    blocks = length // BLOCK

    def per_head(array, width):
        return array.reshape(blocks, BLOCK, ATTENTION_UNITS, width)

    queries = unit_rows(per_head(query_proj, DK).astype(jnp.float32).transpose(0, 2, 1, 3))
    key_rows = unit_rows(per_head(key_proj, DK).astype(jnp.float32).transpose(0, 2, 1, 3))
    values = per_head(value_proj, DV).astype(jnp.float32).transpose(0, 2, 1, 3)
    decays = log_decay.reshape(blocks, BLOCK, ATTENTION_UNITS).transpose(0, 2, 1)
    write_rates = write_rate.reshape(blocks, BLOCK, ATTENTION_UNITS).transpose(0, 2, 1)
    terms = block_terms(queries, key_rows, values, decays, write_rates)
    identity_mat = jnp.broadcast_to(jnp.eye(DK, dtype=jnp.float32), (ATTENTION_UNITS, DK, DK))
    empty_state = jnp.zeros((ATTENTION_UNITS, DK, DV), jnp.float32)

    def block_map(erase, insert, carried_keys, retention):
        step_map = retention * identity_mat - left_contract(carried_keys, erase)
        step_shift = left_contract(carried_keys, insert)
        return (step_map, step_shift)

    def compose_block(carry, pieces):
        step_map, step_shift = block_map(pieces[0], pieces[1], pieces[2], pieces[3])
        return ((matmul(step_map, carry[0]), matmul(step_map, carry[1]) + step_shift), None)

    first_map = block_map(terms[0][0], terms[1][0], terms[2][0], terms[5][0])
    own_map, unused = lax.scan(
        compose_block, first_map, (terms[0][1:], terms[1][1:], terms[2][1:], terms[5][1:])
    )
    prefix = prefix_2((own_map[0], own_map[1]), "seq", compose, (identity_mat, empty_state))
    through = compose(prefix, own_map)
    joined = spread_2(
        jnp.concatenate([through[0], through[1]], axis=-1), "seq", lax.axis_size("seq") - 1
    )
    group_map = (joined[..., :DK], joined[..., DK:])
    earlier_groups = prefix_2(
        (group_map[0], group_map[1]), "grp", compose, (identity_mat, empty_state)
    )
    group_start = apply_map(earlier_groups, initial_state)
    start_state = apply_map(prefix, group_start)

    def advance(state, pieces):
        readout, next_state = block_apply(pieces, state)
        return (next_state, readout)

    final_state, readouts = lax.scan(advance, start_state, terms)
    mixed = gated_norm(readouts.transpose(0, 2, 1, 3), per_head(gate_proj, DV), norm_gain)
    return mixed.reshape(length, ATTENTION_UNITS * DV)


def solution(mesh):
    placed = (
        P(("grp", "seq"), None),
        P(("grp", "seq"), None),
        P(("grp", "seq"), None),
        P(("grp", "seq"), None),
        P(("grp", "seq"), None),
        P(("grp", "seq"), None),
        P(),
        P(),
    )
    return jax.shard_map(
        body, mesh=mesh, in_specs=placed, out_specs=P(("grp", "seq"), None), check_vma=False
    )
```

profile of v0, /device:TPU:0, one launch (start us, length us, event | category | flops | bytes accessed | tf_op | source)
XLA Modules:
  0.0 640.8 jit_solution(17351894979287370236)
XLA Ops:
  10.1 3.8 fusion.43
  13.9 158.8 %custom-call.3 = f32[2,16,1,64,64]{3,4,2,1,0:T(8,128)} custom-call(f32[2,16,1,64,64]{4,3,2,1,0:T(8,128)} %fusion.43), custom_call_target="InvertDiagBlocksLowerTriangular" | custom-call | tf_op jit(solution)/shard_map/triangular_solve | solution.py:66
  188.4 2.9 convolution_subtract_fusion.1
  193.5 79.5 %all-gather.11.cloned.1.call-done = f32[128,128,128]{2,1,0:T(8,128)} async-done(((f32[16,128,128]{2,1,0:T(8,128)}), f32[128,128,128]{2,1,0:T(8,128)}) %all-gather.11.cloned.1.call-update) | async-done | bytes 8388624 | tf_op jit(solution)/shard_map/all_gather | solution.py:17
  273.0 82.2 %all-gather.9.cloned.1.call-done = f32[128,128,128]{2,1,0:T(8,128)} async-done(((f32[16,128,128]{2,1,0:T(8,128)}), f32[128,128,128]{2,1,0:T(8,128)}) %all-gather.9.cloned.1.call-update) | async-done | bytes 8388624 | tf_op jit(solution)/shard_map/all_gather | solution.py:17
  355.2 43.8 %while.50 = (s32[]{:T(128)}, f32[16,128,128]{2,1,0:T(8,128)S(1)}, f32[16,128,128]{2,1,0:T(8,128)S(1)}, s32[]{:T(128)}, f32[8,16,128,128]{3,2,1,0:T(8,128)}, /*in...) while((s32[]{:T(128)}, f32[16,128,128]{2,1,0:T(8,128)S(1)}, f32[16,128,128]{2,1,0:T(8,128)S(1)}, ...), condition=%wide.region_3.4_spmd.clone, body=%wide.region_2.0_spmd.clone.sunk | while | flops 806617088 | bytes 13634664 | solution.py:27
  355.3 2.8 fusion.127
  360.8 2.8 fusion.127
  366.3 2.8 fusion.127
  371.8 2.8 fusion.127
  382.7 2.8 fusion.127
  388.2 2.8 fusion.127
  393.6 2.8 fusion.127
  399.1 3.5 fusion.74
  406.0 63.7 %all-reduce.2.cloned.1.call-done = f32[16,128,256]{1,2,0:T(8,128)} async-done(((f32[16,128,256]{1,2,0:T(8,128)}), f32[16,128,256]{1,2,0:T(8,128)}) %all-reduce.2.cloned.1.call-update) | async-done | bytes 2097168 | tf_op jit(solution)/shard_map/psum | solution.py:32
  484.1 3.4 convolution_multiply_fusion
  487.5 39.8 %all-gather.13.cloned.1.call-done = f32[64,128,128]{2,1,0:T(8,128)} async-done(((f32[16,128,128]{2,1,0:T(8,128)}), f32[64,128,128]{2,1,0:T(8,128)}) %all-gather.13.cloned.1.call-update) | async-done | bytes 4194320 | tf_op jit(solution)/shard_map/all_gather | solution.py:17
  527.3 54.3 %all-gather.15.cloned.1.call-done = f32[64,128,128]{2,1,0:T(8,128)} async-done(((f32[16,128,128]{2,1,0:T(8,128)}), f32[64,128,128]{2,1,0:T(8,128)}) %all-gather.15.cloned.1.call-update) | async-done | bytes 4194320 | tf_op jit(solution)/shard_map/all_gather | solution.py:17
  581.7 30.3 %while.51 = (s32[]{:T(128)}, f32[16,128,128]{2,1,0:T(8,128)S(1)}, f32[16,128,128]{2,1,0:T(8,128)}, s32[]{:T(128)}, f32[4,16,128,128]{3,2,1,0:T(8,128)}, /*index=5*/f32[4,16,128,128]{3,2,1,0:T(8,128)}, s32[]{:T(128)}, s32[]{:T(128)}) while((s32[]{:T(128)}, f32[16,128,128]{2,1,0:T(8,128)S(1)}, f32[16,128,128]{2,1,0:T(8,128)}, ...), condition=%wide.region_6.7_spmd.clone, body=%wide.region_5.6_spmd.clone.sunk | while | flops 806617088 | bytes 13634664 | solution.py:27
  583.0 3.8 fusion.132
  590.5 3.8 fusion.132
  598.1 3.8 fusion.132
  605.7 3.8 fusion.132
  615.8 13.6 %while.49 = (s32[]{:T(128)}, f32[16,128,128]{2,1,0:T(8,128)S(1)}, f32[2,16,64,128]{3,1,2,0:T(8,128)}, f32[2,16,1,1]{1,3,2,0:T(1,128)S(1)}, f32[2,16,64,128]{3,2,...) while((s32[]{:T(128)}, f32[16,128,128]{2,1,0:T(8,128)S(1)}, ...), condition=%wide.region_9.10_spmd, body=%wide.region_8.9_spmd.sunk | while | flops 705429504 | bytes 30934916 | solution.py:151
  (163 shorter events, 99.3 us)
Async XLA Ops:
  6.5 605.5 %copy-start = (f32[16,128,128]{2,1,0:T(8,128)S(1)}, f32[16,128,128]{2,1,0:T(8,128)}, u32[]{:S(2)}) copy-start(f32[16,128,128]{2,1,0:T(8,128)} %param.21) | copy-start | bytes 3145732
  6.5 266.5 %all-gather.11.cloned.1.call-start = ((), (), s32[]{:S(2)}) async-start(), calls=%async_computation.2 | async-start | bytes 9437184 | tf_op jit(solution)/shard_map/all_gather | solution.py:17
  8.1 1.7 copy-start.17
  9.5 164.1 %copy-start.7 = (f32[16,8,16,128]{3,2,1,0:T(8,128)}, f32[16,8,16,128]{3,2,1,0:T(8,128)S(1)}, u32[]{:S(2)}) copy-start(f32[16,8,16,128]{3,2,1,0:T(8,128)S(1)} %copy.80) | copy-start | bytes 3145732
  10.1 162.6 %copy-start.16 = (bf16[128,2048]{1,0:T(8,128)(2,1)S(1)}, bf16[128,2048]{1,0:T(8,128)(2,1)}, u32[]{:S(2)}) copy-start(bf16[128,2048]{1,0:T(8,128)(2,1)} %param.16) | copy-start | bytes 1572868
  174.4 13.9 %copy-start.3 = (f32[2,16,64,128]{3,2,1,0:T(8,128)}, f32[2,16,64,128]{3,2,1,0:T(8,128)S(1)}, u32[]{:S(2)}) copy-start(f32[2,16,64,128]{3,2,1,0:T(8,128)S(1)} %get-tuple-element.647) | copy-start | bytes 3145732
  176.6 6.1 copy-start.5
  188.1 167.1 %all-gather.9.cloned.1.call-start = ((), (), s32[]{:S(2)}) async-start(), calls=%async_computation.1 | async-start | bytes 9437184 | tf_op jit(solution)/shard_map/all_gather | solution.py:17
  193.5 276.3 %all-reduce.2.cloned.1.call-start = ((), (), s32[]{:S(2)}) async-start(), calls=%async_computation | async-start | bytes 4194304 | tf_op jit(solution)/shard_map/psum | solution.py:32
  399.0 5.4 copy-start.1
  399.0 3.5 copy-start.9
  399.0 3.5 copy-start.12
  406.0 121.4 %all-gather.13.cloned.1.call-start = ((), (), s32[]{:S(2)}) async-start(), calls=%async_computation.3 | async-start | bytes 5242880 | tf_op jit(solution)/shard_map/all_gather | solution.py:17
  475.0 106.6 %all-gather.15.cloned.1.call-start = ((), (), s32[]{:S(2)}) async-start(), calls=%async_computation.4 | async-start | bytes 5242880 | tf_op jit(solution)/shard_map/all_gather | solution.py:17
  478.4 2.5 copy-start.6
  482.5 1.6 copy-start.8
  612.0 2.6 copy-start.2
  615.8 15.2 %copy-start.18 = (f32[128]{0:T(128)S(1)}, f32[128]{0:T(128)}, u32[]{:S(2)}) copy-start(f32[128]{0:T(128)} %param.20) | copy-start | bytes 1540
  615.8 2.4 copy-start.10
  615.8 3.1 copy-start.11
  620.5 2.0 copy-start.14
  622.6 2.4 copy-start.10
  622.6 3.1 copy-start.11
  627.3 2.0 copy-start.14
  (5 other events, 6.9 us)
Sparse Core Ops, SparseCore 0:
  188.2 84.7 all-gather.10
  274.6 80.5 all-gather.8
  406.1 63.5 all-reduce.1
  475.1 52.1 all-gather.12
  529.0 52.5 all-gather.14
where the time goes:
time: 645 us; the launch traced here: 641 us
  waiting for transfers between devices  320 us (50%)
  other arithmetic  172 us (27%)
  matrix products  112 us (17%)
  local copies, waits for them, and re-layouts  22.5 us (3%)
  between operations  14 us (2%)
    all_gather x4, waiting for transfers between devices, prefix_2(): everything = jax.tree.map(lambda part: lax.all_gather(part, axis), x)  256 us
    another operation x4, other arithmetic, block_terms(): lax.linalg.triangular_solve(unit_lower, stacked, left_side=True, lower=Tr...  159 us
    dot_general x36, matrix products, matmul(): return jnp.einsum('...ij,...jk->...ik', left, right, precision=HIGHEST)  89.1 us
    psum x1, waiting for transfers between devices, spread_2(): return lax.psum(jnp.where(mine, x, jnp.zeros_like(x)), axis)  63.7 us
    dot_general x6, matrix products, left_contract(): return jnp.einsum('...ci,...cj->...ij', left, right, precision=HIGHEST)  13.4 us
  transfers between devices with their start and end apart: 5, of which 5 were waited for; matrix products, arithmetic and copies ran while one was open for 3% of the time, Pallas kernels for 0%

commit v1 on v0

v1 whole, which is shorter than its diff:
```python
import functools

import jax
import jax.numpy as jnp
from jax import lax
from jax.experimental import pallas as pl
from jax.experimental.pallas import tpu as pltpu
from jax.sharding import PartitionSpec as P

ATTENTION_UNITS = 16
DK = 128
DV = 128
HALF = ATTENTION_UNITS // 2
F32 = jnp.float32
BF16 = jnp.bfloat16
HIGHEST = lax.Precision.HIGHEST
VMEM_LIMIT = 60 * 1024 * 1024


def dot(left, right):
    return jnp.dot(left, right, preferred_element_type=F32)


def dot_t(left, right):
    return lax.dot_general(left, right, (((1,), (1,)), ((), ())), preferred_element_type=F32)


def t_dot(left, right):
    return lax.dot_general(left, right, (((0,), (0,)), ((), ())), preferred_element_type=F32)


def split(x):
    high = x.astype(BF16)
    low = (x - high.astype(F32)).astype(BF16)
    return high, low


def wide(x):
    return jnp.concatenate(split(x), axis=1)


def halves_sum(x):
    width = x.shape[1] // 2
    return x[:, :width] + x[:, width:]


def mul(left, right):
    pair = wide(left)
    high, low = split(right)
    if right.shape[1] == DK:
        row = jnp.concatenate([high, low], axis=1)
        return halves_sum(dot(pair, jnp.concatenate([row, row], axis=0)))
    return dot(pair, jnp.concatenate([high, high], axis=0)) + dot(
        pair, jnp.concatenate([low, low], axis=0)
    )


def mul_exact(left, right):
    return dot(wide(left), jnp.concatenate([right, right], axis=0))


def positions(size):
    later = lax.broadcasted_iota(jnp.int32, (size, size), 0)
    earlier = lax.broadcasted_iota(jnp.int32, (size, size), 1)
    return later, earlier


def three(x):
    first = x.astype(BF16)
    rest = x - first.astype(F32)
    second = rest.astype(BF16)
    third = (rest - second.astype(F32)).astype(BF16)
    return first, second, third


def running_sum(decays):
    later, earlier = positions(decays.shape[0])
    ones = jnp.where(later >= earlier, 1.0, 0.0).astype(BF16)
    first, second, third = three(decays)
    return dot(ones, first) + (dot(ones, second) + dot(ones, third))


def pick_half(x, side, axis):
    low = lax.slice_in_dim(x, 0, HALF, axis=axis)
    high = lax.slice_in_dim(x, HALF, 2 * HALF, axis=axis)
    return jnp.where(side == 0, low, high)


def map_kernel(side_ref, key_ref, value_ref, decay_ref, rate_ref, maps_ref, solved_ref):
    side = side_ref[0]
    length = key_ref.shape[0]
    later, earlier = positions(length)
    eye = later == earlier
    identity = jnp.where(eye, 1.0, 0.0)
    total = running_sum(decay_ref[...])
    rates = rate_ref[...]
    total_col = pick_half(total, side, 1)
    rate_col = pick_half(rates, side, 1)
    total_row = pick_half(total.T, side, 0)
    rate_row = pick_half(rates.T, side, 0)
    heads = range(HALF)
    keys = [key_ref[:, h * DK : (h + 1) * DK] for h in heads]
    values = [value_ref[:, h * DV : (h + 1) * DV] for h in heads]
    grams = [dot_t(keys[h], keys[h]) for h in heads]
    lower, unit_row, unit_col = [], [], []
    for h in heads:
        diagonal = jnp.where(eye, grams[h], 0.0)
        row = lax.rsqrt(jnp.sum(diagonal, axis=0, keepdims=True) + 1e-06)
        col = lax.rsqrt(jnp.sum(diagonal, axis=1, keepdims=True) + 1e-06)
        spread = total_col[:, h : h + 1] - total_row[h : h + 1, :]
        strict = later > earlier
        damping = jnp.exp(jnp.where(strict, spread, 0.0))
        scale = (rate_col[:, h : h + 1] * col) * row
        lower.append(jnp.where(strict, grams[h] * scale * damping, 0.0))
        unit_row.append(row)
        unit_col.append(col)
    size = 1
    inverse = [
        identity - jnp.where((later // 2) == (earlier // 2), lower[h], 0.0) for h in heads
    ]
    size = 2
    while size < length:
        band = ((later // (2 * size)) == (earlier // (2 * size))) & (
            (later // size) != (earlier // size)
        )
        inner = [mul(jnp.where(band, lower[h], 0.0), inverse[h]) for h in heads]
        outer = [mul(inverse[h], inner[h]) for h in heads]
        inverse = [inverse[h] - outer[h] for h in heads]
        size *= 2
    for h in heads:
        row = total_row[h : h + 1, :]
        rate = rate_row[h : h + 1, :]
        erase = mul_exact(inverse[h] * (rate * jnp.exp(row) * unit_row[h]), keys[h])
        insert = mul_exact(inverse[h] * rate, values[h])
        solved = jnp.concatenate([erase, insert], axis=1)
        solved_ref[h] = solved
        final = total_col[length - 1 : length, h : h + 1]
        carried = jnp.exp(final - total_col[:, h : h + 1]) * unit_col[h]
        high, low = split(solved * carried)
        moved = t_dot(keys[h], high) + t_dot(keys[h], low)
        maps_ref[h, :, :DK] = jnp.exp(final) * identity - moved[:, :DK]
        maps_ref[h, :, DK:] = moved[:, DK:]


def whole(shape):
    return pl.BlockSpec(shape, lambda i, *refs: (0,) * len(shape))


def params():
    return pltpu.CompilerParams(vmem_limit_bytes=VMEM_LIMIT)


def make_maps(side, keys, values, decays, rates):
    length = keys.shape[0]
    block = pl.BlockSpec((length, HALF * DK), lambda i, side: (0, side[0]))
    out = jax.ShapeDtypeStruct((HALF, DK, DK + DV), F32)
    solved = jax.ShapeDtypeStruct((HALF, length, DK + DV), F32)
    return pl.pallas_call(
        map_kernel,
        out_shape=(out, solved),
        grid_spec=pltpu.PrefetchScalarGridSpec(
            num_scalar_prefetch=1,
            grid=(1,),
            in_specs=[block, block, whole(decays.shape), whole(rates.shape)],
            out_specs=(whole(out.shape), whole(solved.shape)),
        ),
        compiler_params=params(),
        name="block_maps",
    )(side, keys, values, decays, rates)


def readout_kernel(side_ref, query_ref, key_ref, decay_ref, solved_ref, from_state_ref, own_ref):
    side = side_ref[0]
    length = key_ref.shape[0]
    later, earlier = positions(length)
    total = running_sum(decay_ref[...])
    total_col = pick_half(total, side, 1)
    total_row = pick_half(total.T, side, 0)
    within = later >= earlier
    for h in range(HALF):
        query = query_ref[:, h * DK : (h + 1) * DK]
        key = key_ref[:, h * DK : (h + 1) * DK]
        wide_query = query.astype(F32)
        wide_key = key.astype(F32)
        query_unit = lax.rsqrt(jnp.sum(wide_query * wide_query, axis=1, keepdims=True) + 1e-06)
        key_unit = lax.rsqrt(jnp.sum(wide_key * wide_key, axis=1, keepdims=True) + 1e-06)
        key_row = jnp.broadcast_to(key_unit, (length, DK)).T[:1, :]
        spread = total_col[:, h : h + 1] - total_row[h : h + 1, :]
        damping = jnp.exp(jnp.where(within, spread, 0.0))
        mix = jnp.where(within, dot_t(query, key) * damping * query_unit * key_row, 0.0)
        product = mul(mix, solved_ref[h])
        grown = jnp.exp(total_col[:, h : h + 1]) * query_unit
        from_state_ref[h] = grown * wide_query - product[:, :DK]
        own_ref[h] = product[:, DK:]


def make_readout(side, queries, keys, decays, solved):
    length = keys.shape[0]
    block = pl.BlockSpec((length, HALF * DK), lambda i, side: (0, side[0]))
    out = jax.ShapeDtypeStruct((HALF, length, DK), F32)
    own = jax.ShapeDtypeStruct((HALF, length, DV), F32)
    return pl.pallas_call(
        readout_kernel,
        out_shape=(out, own),
        grid_spec=pltpu.PrefetchScalarGridSpec(
            num_scalar_prefetch=1,
            grid=(1,),
            in_specs=[block, block, whole(decays.shape), whole(solved.shape)],
            out_specs=(whole(out.shape), whole(own.shape)),
        ),
        compiler_params=params(),
        name="readout_terms",
    )(side, queries, keys, decays, solved)


def finish_kernel(side_ref, from_state_ref, own_ref, state_ref, gate_ref, gain_ref, *rest):
    out_ref = rest[-1]
    gain = gain_ref[...]
    for h in range(HALF):
        readout = own_ref[h] + mul(from_state_ref[h], state_ref[h])
        mean = jnp.mean(readout * readout, axis=1, keepdims=True)
        gate = gate_ref[:, h * DV : (h + 1) * DV].astype(F32)
        scaled = readout * lax.rsqrt(mean + 1e-05) * gain
        gated = scaled * (gate / (1.0 + jnp.exp(-gate)))
        out_ref[:, h * DV : (h + 1) * DV] = gated.astype(BF16)


def finish(side, from_state, own, state, gate, gain, before=None):
    length = gate.shape[0]
    block = pl.BlockSpec((length, HALF * DV), lambda i, side: (0, side[0]))
    specs = [whole(from_state.shape), whole(own.shape), whole(state.shape), block, whole((1, DV))]
    operands = [side, from_state, own, state, gate, gain]
    aliases = {}
    if before is not None:
        specs.append(pl.BlockSpec(memory_space=pl.ANY))
        operands.append(before)
        aliases = {6: 0}
    return pl.pallas_call(
        finish_kernel,
        out_shape=jax.ShapeDtypeStruct(gate.shape, BF16),
        grid_spec=pltpu.PrefetchScalarGridSpec(
            num_scalar_prefetch=1, grid=(1,), in_specs=specs, out_specs=block
        ),
        input_output_aliases=aliases,
        compiler_params=params(),
        name="gated_readout",
    )(*operands)


def compose_into(later, earlier):
    both = mul(later[:, :DK], earlier)
    return both[:, :DK], both[:, DK:] + later[:, DK:]


def chip_kernel(place_ref, own_ref, other_ref, *out_refs):
    core, z = place_ref[0], place_ref[1]
    rounds = len(out_refs)
    share = HALF // rounds

    def go(first_ref, second_ref):
        for r, out_ref in enumerate(out_refs):
            base = (z ^ r) * share
            for i in range(share):
                a, b = compose_into(second_ref[base + i], first_ref[base + i])
                out_ref[i, :, :DK] = a
                out_ref[i, :, DK:] = b

    @pl.when(core == 0)
    def _():
        go(own_ref, other_ref)

    @pl.when(core != 0)
    def _():
        go(other_ref, own_ref)


def chip_maps(place, own, other, rounds):
    out = jax.ShapeDtypeStruct((HALF // rounds, DK, DK + DV), F32)
    return pl.pallas_call(
        chip_kernel,
        out_shape=(out,) * rounds,
        grid_spec=pltpu.PrefetchScalarGridSpec(
            num_scalar_prefetch=1,
            grid=(1,),
            in_specs=[whole(own.shape), whole(other.shape)],
            out_specs=(whole(out.shape),) * rounds,
        ),
        compiler_params=params(),
        name="chip_maps",
    )(place, own, other)


def group_kernel(place_ref, *refs):
    z = place_ref[1]
    rounds = len(refs) - 2
    in_refs, total_ref, prefix_ref = refs[:rounds], refs[rounds], refs[rounds + 1]
    share = total_ref.shape[0]
    for r, ref in enumerate(in_refs):
        prefix_ref[z ^ r] = ref[...]
    for i in range(share):
        running = prefix_ref[0, i]
        for k in range(1, rounds):
            later = prefix_ref[k, i]
            prefix_ref[k - 1, i] = running
            running = jnp.concatenate(compose_into(later, running), axis=1)
        total_ref[i] = running


def group_maps(place, pieces):
    shape = pieces[0].shape
    out = jax.ShapeDtypeStruct(shape, F32)
    prefix = jax.ShapeDtypeStruct((len(pieces),) + shape, F32)
    return pl.pallas_call(
        group_kernel,
        out_shape=(out, prefix),
        grid_spec=pltpu.PrefetchScalarGridSpec(
            num_scalar_prefetch=1,
            grid=(1,),
            in_specs=[whole(shape)] * len(pieces),
            out_specs=(whole(shape), whole(prefix.shape)),
        ),
        compiler_params=params(),
        name="group_maps",
    )(place, *pieces)


def state_kernel(place_ref, initial_ref, prefix_ref, *refs):
    z, group = place_ref[1], place_ref[2]
    rounds = prefix_ref.shape[0]
    scratch_ref = refs[-1]
    out_refs = refs[-1 - rounds : -1]
    in_refs = refs[: -1 - rounds]
    share = initial_ref.shape[0]
    for r, ref in enumerate(in_refs):
        scratch_ref[group ^ r] = ref[...]

    def advance(k, states):
        return tuple(
            mul(scratch_ref[k, i, :, :DK], states[i]) + scratch_ref[k, i, :, DK:]
            for i in range(share)
        )

    start = lax.fori_loop(0, group, advance, tuple(initial_ref[i] for i in range(share)))
    for r, out_ref in enumerate(out_refs):
        where = z ^ r
        back = jnp.maximum(where - 1, 0)
        for i in range(share):
            moved = mul(prefix_ref[back, i, :, :DK], start[i]) + prefix_ref[back, i, :, DK:]
            out_ref[i] = jnp.where(where == 0, start[i], moved)


def chip_states(place, initial, prefix, groups):
    rounds, share = prefix.shape[:2]
    out = jax.ShapeDtypeStruct((share, DK, DV), F32)
    piece = (share, DK, DK + DV)
    slots = HALF // share
    return pl.pallas_call(
        state_kernel,
        out_shape=(out,) * rounds,
        grid_spec=pltpu.PrefetchScalarGridSpec(
            num_scalar_prefetch=1,
            grid=(1,),
            in_specs=[
                pl.BlockSpec(
                    (share, DK, DV), lambda i, place: (place[0] * slots + place[1], 0, 0)
                ),
                whole(prefix.shape),
            ]
            + [whole(piece)] * len(groups),
            out_specs=(whole(out.shape),) * rounds,
            scratch_shapes=[pltpu.VMEM((len(groups),) + piece, F32)],
        ),
        compiler_params=params(),
        name="chip_states",
    )(place, initial, prefix, *groups)


def core_kernel(place_ref, own_ref, other_ref, *refs):
    core, z = place_ref[0], place_ref[1]
    keep_ref, give_ref = refs[-2:]
    in_refs = refs[:-2]
    share = in_refs[0].shape[0]

    def go(first_ref, start_ref, later_ref):
        for r, ref in enumerate(in_refs):
            base = (z ^ r) * share
            for i in range(share):
                state = ref[i]
                start_ref[base + i] = state
                later_ref[base + i] = (
                    mul(first_ref[base + i, :, :DK], state) + first_ref[base + i, :, DK:]
                )

    @pl.when(core == 0)
    def _():
        go(own_ref, keep_ref, give_ref)

    @pl.when(core != 0)
    def _():
        go(other_ref, give_ref, keep_ref)


def core_states(place, own, other, pieces):
    out = jax.ShapeDtypeStruct((HALF, DK, DV), F32)
    return pl.pallas_call(
        core_kernel,
        out_shape=(out, out),
        grid_spec=pltpu.PrefetchScalarGridSpec(
            num_scalar_prefetch=1,
            grid=(1,),
            in_specs=[whole(own.shape), whole(other.shape)]
            + [whole(pieces[0].shape)] * len(pieces),
            out_specs=(whole(out.shape), whole(out.shape)),
        ),
        compiler_params=params(),
        name="core_states",
    )(place, own, other, *pieces)


def matmul(left, right):
    return jnp.einsum("...ij,...jk->...ik", left, right, precision=HIGHEST)


def gathered_states(maps, initial):
    seq, grp = lax.axis_size("seq"), lax.axis_size("grp")
    place, group = lax.axis_index("seq"), lax.axis_index("grp")

    def compose(before, step):
        both = matmul(step[..., :DK], before)
        return both.at[..., DK:].add(step[..., DK:])

    heads = maps.shape[0]
    identity = jnp.concatenate(
        [jnp.eye(DK, dtype=F32), jnp.zeros((DK, DV), F32)], axis=1
    )
    identity = jnp.broadcast_to(identity, (heads, DK, DK + DV))
    everything = lax.all_gather(maps, "seq")

    def lap(k, carry):
        total, mine = carry
        mine = jnp.where(k == place, total, mine)
        return compose(total, everything[k]), mine

    total, mine = lax.fori_loop(0, seq, lap, (identity, identity))
    groups = lax.all_gather(total, "grp")

    def step(k, state):
        return matmul(groups[k][..., :DK], state) + groups[k][..., DK:]

    start = lax.fori_loop(0, group, step, initial)
    return matmul(mine[..., :DK], start) + mine[..., DK:]


def swap_pairs(size, bit):
    return [(i, i ^ bit) for i in range(size)]


def body(
    query_proj, key_proj, value_proj, log_decay, write_rate, gate_proj, norm_gain, initial_state
):
    seq, grp = lax.axis_size("seq"), lax.axis_size("grp")
    chips = seq // 2
    place = lax.axis_index("seq")
    core, z, group = place % 2, place // 2, lax.axis_index("grp")
    gain = norm_gain.reshape(1, DV)
    mine = core.reshape(1).astype(jnp.int32)
    theirs = 1 - mine
    fast = seq % 2 == 0 and chips in (1, 2, 4, 8) and grp & (grp - 1) == 0

    maps_theirs, solved_theirs = make_maps(theirs, key_proj, value_proj, log_decay, write_rate)
    if not fast:
        maps_mine, solved_mine = make_maps(mine, key_proj, value_proj, log_decay, write_rate)
        maps = jnp.where(
            core == 0,
            jnp.concatenate([maps_mine, maps_theirs]),
            jnp.concatenate([maps_theirs, maps_mine]),
        )
        state = gathered_states(maps, initial_state)
        state_mine = lax.dynamic_slice_in_dim(state, core * HALF, HALF)
        state_theirs = lax.dynamic_slice_in_dim(state, (1 - core) * HALF, HALF)
        terms_mine = make_readout(mine, query_proj, key_proj, log_decay, solved_mine)
        terms_theirs = make_readout(theirs, query_proj, key_proj, log_decay, solved_theirs)
    else:
        spot = jnp.stack([core, z, group]).astype(jnp.int32)
        other = lax.ppermute(maps_theirs, "seq", swap_pairs(seq, 1))
        maps_mine, solved_mine = make_maps(mine, key_proj, value_proj, log_decay, write_rate)
        chip = chip_maps(spot, maps_mine, other, chips)
        pieces = [chip[0]] + [
            lax.ppermute(chip[r], "seq", swap_pairs(seq, 2 * r)) for r in range(1, chips)
        ]
        terms_mine = make_readout(mine, query_proj, key_proj, log_decay, solved_mine)
        terms_theirs = make_readout(theirs, query_proj, key_proj, log_decay, solved_theirs)
        total, prefix = group_maps(spot, pieces)
        groups = [total] + [
            lax.ppermute(total, "grp", swap_pairs(grp, r)) for r in range(1, grp)
        ]
        starts = chip_states(spot, initial_state, prefix, groups)
        back = [starts[0]] + [
            lax.ppermute(starts[r], "seq", swap_pairs(seq, 2 * r)) for r in range(1, chips)
        ]
        state_mine, give = core_states(spot, maps_mine, other, back)
        state_theirs = lax.ppermute(give, "seq", swap_pairs(seq, 1))

    out = finish(mine, *terms_mine, state_mine, gate_proj, gain)
    return finish(theirs, *terms_theirs, state_theirs, gate_proj, gain, out)


def solution(mesh):
    spread = P(("grp", "seq"), None)
    placed = (spread,) * 6 + (P(), P())
    return jax.shard_map(body, mesh=mesh, in_specs=placed, out_specs=spread, check_vma=False)
```

time: 645 us -> 106 us (0.16)
  waiting for transfers between devices: 320 us -> 39.8 us
  other arithmetic: 172 us -> 0.67 us
  matrix products: 112 us -> 0 us
  Pallas kernels: 0 us -> 40.7 us
  starting transfers between devices: 0.38 us -> 17.7 us
  local copies, waits for them, and re-layouts: 22.5 us -> 6.12 us
  between operations: 14 us -> 0.04 us
    all_gather x4 -> x0, waiting for transfers between devices: 256 us -> none  [prefix_2(): everything = jax.tree.map(lambda part: lax.all_gather(part, axis), x)]
    another operation x5 -> x1, other arithmetic: 159 us -> 0.67 us  [body(): spot = jnp.stack([core, z, group]).astype(jnp.int32)]
    dot_general x44 -> x0, matrix products: 110 us -> none  [the longest x36 89.1 us: matmul(): return jnp.einsum('...ij,...jk->...ik', left, right, precision=HIGHEST)]
    psum x1 -> x0, waiting for transfers between devices: 63.7 us -> none  [spread_2(): return lax.psum(jnp.where(mine, x, jnp.zeros_like(x)), axis)]
    pallas_call x0 -> x10, Pallas kernels: none -> 40.7 us  [the longest x2 12.8 us: make_maps(): pl.pallas_call(map_kernel, out_shape=(out, solved), grid_spec=pltpu.Prefe...]
    ppermute x0 -> x11, waiting for transfers between devices: none -> 39.8 us  [the longest x3 19 us: body(): lax.ppermute(chip[r], 'seq', swap_pairs(seq, 2 * r))]
    ppermute x0 -> x11, starting transfers between devices: none -> 17.7 us  [the longest x3 8.53 us: body(): lax.ppermute(starts[r], 'seq', swap_pairs(seq, 2 * r))]
    slice x5 -> x0, local copies, waits for them, and re-layouts: 8.33 us -> none  [the longest x3 6.58 us: body(): group_map = (joined[..., :DK], joined[..., DK:])]
  transfers between devices with their start and end apart: 5 -> 11, of which waited for: 5 -> 7; matrix products, arithmetic and copies ran while one was open for 3% -> 1% of each run, Pallas kernels for 0% -> 16%
where the time goes in v1:
time: 106 us; the launch traced here: 105 us
  Pallas kernels  40.7 us (38%)
  waiting for transfers between devices  39.8 us (38%)
  starting transfers between devices  17.7 us (17%)
  local copies, waits for them, and re-layouts  6.12 us (6%)
    ppermute x3, waiting for transfers between devices, body(): lax.ppermute(chip[r], 'seq', swap_pairs(seq, 2 * r))  19 us
    pallas_call x2, Pallas kernels, make_maps(): pl.pallas_call(map_kernel, out_shape=(out, solved), grid_spec=pltpu.Prefe...  12.8 us
    ppermute x3, waiting for transfers between devices, body(): lax.ppermute(starts[r], 'seq', swap_pairs(seq, 2 * r))  10.6 us
    ppermute x3, waiting for transfers between devices, body(): lax.ppermute(total, 'grp', swap_pairs(grp, r))  10.2 us
    ppermute x3, starting transfers between devices, body(): lax.ppermute(starts[r], 'seq', swap_pairs(seq, 2 * r))  8.53 us
    pallas_call x2, Pallas kernels, make_readout(): pl.pallas_call(readout_kernel, out_shape=(out, own), grid_spec=pltpu.Pref...  8.1 us
    unnamed x28, local copies, waits for them, and re-layouts  6.12 us
    pallas_call x2, Pallas kernels, finish(): pl.pallas_call(finish_kernel, out_shape=jax.ShapeDtypeStruct(gate.shape,...  5.26 us
  transfers between devices with their start and end apart: 11, of which 7 were waited for; matrix products, arithmetic and copies ran while one was open for 1% of the time, Pallas kernels for 16%

profile of v1, /device:TPU:0, one launch (start us, length us, event | category | flops | bytes accessed | tf_op | source)
XLA Modules:
  0.0 104.9 jit_solution(9489712302211795374)
XLA Ops:
  2.1 6.4 %block_maps.2 = (f32[8,128,256]{2,1,0:T(8,128)}, f32[8,128,256]{2,1,0:T(8,128)}) custom-call(s32[1]{0:T(128)S(6)} %sub.7.side_ref, bf16[128,2048]{1,0:T(8,128)(2,1)} %key_ref.7, bf16[128,2048]{1,0:T(8,128)(2,1)} %value_ref.3, f32[128,16]{1,0:T(8,128)} %copy.12.decay_ref, f32[128,16]{1,0:T(8,128)} %copy.11.rate_ref), custom_call_target="tpu_custom_call" | custom-call | tf_op jit(solution)/shard_map/block_maps/pallas_call | solution.py:158
  9.0 6.4 %block_maps.3 = (f32[8,128,256]{2,1,0:T(8,128)}, f32[8,128,256]{2,1,0:T(8,128)}) custom-call(s32[1]{0:T(128)} %bitcast.side_ref, bf16[128,2048]{1,0:T(8,128)(2,1)} %key_ref.7, bf16[128,2048]{1,0:T(8,128)(2,1)} %value_ref.3, f32[128,16]{1,0:T(8,128)} %copy.12.decay_ref, f32[128,16]{1,0:T(8,128)} %copy.11.rate_ref), custom_call_target="tpu_custom_call" | custom-call | tf_op jit(solution)/shard_map/block_maps/pallas_call | solution.py:158
  16.1 1.0 copy-done
  17.0 3.6 %chip_maps.1 = (f32[2,128,256]{2,1,0:T(8,128)}, f32[2,128,256]{2,1,0:T(8,128)}, f32[2,128,256]{2,1,0:T(8,128)}, f32[2,128,256]{2,1,0:T(8,128)}) custom-call(s32[3]{0:T(128)} %pad_add_fusion.place_ref, f32[8,128,256]{2,1,0:T(8,128)} %get-tuple-element.28.own_ref, f32[8,128,256]{2,1,0:T(8,128)} %copy-done), custom_call_target="tpu_custom_call" | custom-call | tf_op jit(solution)/shard_map/chip_maps/pallas_call | solution.py:279
  20.7 2.6 %collective-permute-start.1 = (f32[2,128,256]{2,1,0:T(8,128)}, f32[2,128,256]{2,1,0:T(8,128)S(1)}, u32[]{:S(2)}, u32[]{:S(2)}) collective-permute-start(f32[2,128,256]{2,1,0:T(8,128)} %get-tuple-element.31), channel_id=1, source_target_pairs={{0,2},{1,3},{2,0},{3,1},{4,6},{5,7},{6,4},{7,5},{8,10},{9,11},{10,... | collective-permute-start | bytes 786440 | tf_op jit(solution)/shard_map/ppermute | solution.py:489
  23.2 2.6 %collective-permute-start.2 = (f32[2,128,256]{2,1,0:T(8,128)}, f32[2,128,256]{2,1,0:T(8,128)S(1)}, u32[]{:S(2)}, u32[]{:S(2)}) collective-permute-start(f32[2,128,256]{2,1,0:T(8,128)} %get-tuple-element.32), channel_id=1, source_target_pairs={{0,4},{1,5},{2,6},{3,7},{4,0},{5,1},{6,2},{7,3},{8,12},{9,13},{10,... | collective-permute-start | bytes 786440 | tf_op jit(solution)/shard_map/ppermute | solution.py:489
  25.8 9.8 %collective-permute-done.1.refs_1_ = f32[2,128,256]{2,1,0:T(8,128)S(1)} collective-permute-done((f32[2,128,256]{2,1,0:T(8,128)}, f32[2,128,256]{2,1,0:T(8,128)S(1)}, u32[]{:S(2)}, u32[]{:S(2)}) %collective-permute-start.1) | collective-permute-done | bytes 262176 | tf_op jit(solution)/shard_map/ppermute | solution.py:489
  35.6 9.2 %collective-permute-done.2.refs_2_ = f32[2,128,256]{2,1,0:T(8,128)S(1)} collective-permute-done((f32[2,128,256]{2,1,0:T(8,128)}, f32[2,128,256]{2,1,0:T(8,128)S(1)}, u32[]{:S(2)}, u32[]{:S(2)}) %collective-permute-start.2) | collective-permute-done | bytes 262176 | tf_op jit(solution)/shard_map/ppermute | solution.py:489
  45.6 3.7 %group_maps.1 = (f32[2,128,256]{2,1,0:T(8,128)}, f32[4,2,128,256]{3,2,1,0:T(8,128)}) custom-call(s32[3]{0:T(128)} %pad_add_fusion.place_ref, f32[2,128,256]{2,1,0:T(8,128)} %get-tuple-element.30.refs_0_, f32[2,128,256]{2,1,0:T(8,128)} %copy-done.2, f32[2,128,256]{2,1,0:T(8,128)} %copy-done.3, f32[2,128,256]{2,1,0:T(8,128)} %copy-done.4), custom_call_target="tpu_custom_call" | custom-call | tf_op jit(solution)/shard_map/group_maps/pallas_call | solution.py:313
  49.4 2.4 %collective-permute-start.6 = (f32[2,128,256]{2,1,0:T(8,128)}, f32[2,128,256]{2,1,0:T(8,128)S(1)}, u32[]{:S(2)}, u32[]{:S(2)}) collective-permute-start(f32[2,128,256]{2,1,0:T(8,128)} %get-tuple-element.35.refs_0_), channel_id=1, source_target_pairs={{0,24},{8,16},{16,8},{24,0},{1,25},{9,17},{17,9},{25,1},{2,26},{10... | collective-permute-start | bytes 786440 | tf_op jit(solution)/shard_map/ppermute | solution.py:495
  52.8 6.8 %collective-permute-done.6.refs_3_ = f32[2,128,256]{2,1,0:T(8,128)S(1)} collective-permute-done((f32[2,128,256]{2,1,0:T(8,128)}, f32[2,128,256]{2,1,0:T(8,128)S(1)}, u32[]{:S(2)}, u32[]{:S(2)}) %collective-permute-start.6) | collective-permute-done | bytes 262176 | tf_op jit(solution)/shard_map/ppermute | solution.py:495
  59.7 3.2 %collective-permute-done.5.refs_2_ = f32[2,128,256]{2,1,0:T(8,128)S(1)} collective-permute-done((f32[2,128,256]{2,1,0:T(8,128)}, f32[2,128,256]{2,1,0:T(8,128)S(1)}, u32[]{:S(2)}, u32[]{:S(2)}) %collective-permute-start.5) | collective-permute-done | bytes 262176 | tf_op jit(solution)/shard_map/ppermute | solution.py:495
  63.7 3.3 %chip_states.1 = (f32[2,128,128]{2,1,0:T(8,128)}, f32[2,128,128]{2,1,0:T(8,128)}, f32[2,128,128]{2,1,0:T(8,128)}, f32[2,128,128]{2,1,0:T(8,128)}) custom-call(s32[3]{0:T(128)} %pad_add_fusion.place_ref, f32[16,128,128]{2,1,0:T(8,128)} %initial_ref.1, f32[4,2,128,256]{3,2,1,0:T(8,128)} %get-tuple-element.34.prefix_ref, ...), custom_call_target="tpu_custom_call" | custom-call | tf_op jit(solution)/shard_map/chip_states/pallas_call | solution.py:357
  67.0 6.1 %collective-permute-start.7 = (f32[2,128,128]{2,1,0:T(8,128)}, f32[2,128,128]{2,1,0:T(8,128)S(1)}, u32[]{:S(2)}, u32[]{:S(2)}) collective-permute-start(f32[2,128,128]{2,1,0:T(8,128)} %get-tuple-element.37), channel_id=1, source_target_pairs={{0,2},{1,3},{2,0},{3,1},{4,6},{5,7},{6,4},{7,5},{8,10},{9,11},{10,... | collective-permute-start | bytes 393224 | tf_op jit(solution)/shard_map/ppermute | solution.py:499
  73.1 1.0 collective-permute-start.8
  74.1 1.5 %collective-permute-start.9 = (f32[2,128,128]{2,1,0:T(8,128)}, f32[2,128,128]{2,1,0:T(8,128)S(1)}, u32[]{:S(2)}, u32[]{:S(2)}) collective-permute-start(f32[2,128,128]{2,1,0:T(8,128)} %get-tuple-element.39), channel_id=1, source_target_pairs={{0,6},{1,7},{2,4},{3,5},{4,2},{5,3},{6,0},{7,1},{8,14},{9,15},{10,... | collective-permute-start | bytes 393224 | tf_op jit(solution)/shard_map/ppermute | solution.py:499
  75.6 3.1 %collective-permute-done.7.refs_1_ = f32[2,128,128]{2,1,0:T(8,128)S(1)} collective-permute-done((f32[2,128,128]{2,1,0:T(8,128)}, f32[2,128,128]{2,1,0:T(8,128)S(1)}, u32[]{:S(2)}, u32[]{:S(2)}) %collective-permute-start.7) | collective-permute-done | bytes 131104 | tf_op jit(solution)/shard_map/ppermute | solution.py:499
  78.7 7.5 %collective-permute-done.8.refs_2_ = f32[2,128,128]{2,1,0:T(8,128)S(1)} collective-permute-done((f32[2,128,128]{2,1,0:T(8,128)}, f32[2,128,128]{2,1,0:T(8,128)S(1)}, u32[]{:S(2)}, u32[]{:S(2)}) %collective-permute-start.8) | collective-permute-done | bytes 131104 | tf_op jit(solution)/shard_map/ppermute | solution.py:499
  86.9 3.8 %core_states.1 = (f32[8,128,128]{2,1,0:T(8,128)}, f32[8,128,128]{2,1,0:T(8,128)}) custom-call(s32[3]{0:T(128)} %pad_add_fusion.place_ref, f32[8,128,256]{2,1,0:T(8,128)} %get-tuple-element.28.own_ref, f32[8,128,256]{2,1,0:T(8,128)} %copy-done, f32[2,128,128]{2,1,0:T(8,128)} %get-tuple-element.36.refs_0_, f32[2,128,128]{2,1,0:T(8,128)} %copy-done.8, ...), custom_call_target="tpu_custom_call" | custom-call | tf_op jit(solution)/shard_map/core_states/pallas_call | solution.py:405
  90.7 4.1 %readout_terms.3 = (f32[8,128,128]{2,1,0:T(8,128)}, f32[8,128,128]{2,1,0:T(8,128)}) custom-call(s32[1]{0:T(128)} %bitcast.side_ref, bf16[128,2048]{1,0:T(8,128)(2,1)} %query_ref.3, bf16[128,2048]{1,0:T(8,128)(2,1)} %key_ref.7, f32[128,16]{1,0:T(8,128)} %copy.12.decay_ref, f32[8,128,256]{2,1,0:T(8,128)} %get-tuple-element.41.solved_ref), custom_call_target="tpu_custom_call" | custom-call | tf_op jit(solution)/shard_map/readout_terms/pallas_call | solution.py:202
  94.8 4.0 %readout_terms.2 = (f32[8,128,128]{2,1,0:T(8,128)}, f32[8,128,128]{2,1,0:T(8,128)}) custom-call(s32[1]{0:T(128)S(6)} %sub.7.side_ref, bf16[128,2048]{1,0:T(8,128)(2,1)} %query_ref.3, bf16[128,2048]{1,0:T(8,128)(2,1)} %key_ref.7, f32[128,16]{1,0:T(8,128)} %copy.12.decay_ref, f32[8,128,256]{2,1,0:T(8,128)} %get-tuple-element.25.solved_ref), custom_call_target="tpu_custom_call" | custom-call | tf_op jit(solution)/shard_map/readout_terms/pallas_call | solution.py:202
  98.8 2.6 %gated_readout.2.rest_0_ = bf16[128,2048]{1,0:T(8,128)(2,1)} custom-call(s32[1]{0:T(128)} %bitcast.side_ref, f32[8,128,128]{2,1,0:T(8,128)} %get-tuple-element.42.from_state_ref, f32[8,128,128]{2,1,0:T(8,128)} %get-tuple-element.43.own_ref, f32[8,128,128]{2,1,0:T(8,128)} %get-tuple-element.44.state_ref, bf16[128,2048]{1,0:T(8,128)(2,1)} %gate_ref.3, ...), custom_call_target="tpu_custom_call" | custom-call | tf_op jit(solution)/shard_map/gated_readout/pallas_call | solution.py:238
  101.5 0.8 copy-done.1
  102.3 2.6 %gated_readout.3 = bf16[128,2048]{1,0:T(8,128)(2,1)} custom-call(s32[1]{0:T(128)S(6)} %sub.7.side_ref, f32[8,128,128]{2,1,0:T(8,128)} %get-tuple-element.26.from_state_ref, f32[8,128,128]{2,1,0:T(8,128)} %get-tuple-element.27.own_ref, f32[8,128,128]{2,1,0:T(8,128)} %copy-done.1, bf16[128,2048]{1,0:T(8,128)(2,1)} %gate_ref.3, ...), custom_call_target="tpu_custom_call", output_to_operand_aliasing={{}: (6, {})} | custom-call | tf_op jit(solution)/shard_map/gated_readout/pallas_call | solution.py:238
  (37 shorter events, 6.7 us)
Async XLA Ops:
  0.0 0.7 copy-start.11
  0.7 0.7 copy-start.12
  8.6 7.5 %collective-permute-start = (f32[8,128,256]{2,1,0:T(8,128)}, f32[8,128,256]{2,1,0:T(8,128)S(1)}, u32[]{:S(2)}, u32[]{:S(2)}) collective-permute-start(f32[8,128,256]{2,1,0:T(8,128)} %get-tuple-element.29), channel_id=1, source_target_pairs={{0,1},{1,0},{2,3},{3,2},{4,5},{5,4},{6,7},{7,6},{8,9},{9,8},{10,11... | collective-permute-start | bytes 3145736 | tf_op jit(solution)/shard_map/ppermute | solution.py:485
  16.1 1.0 copy-start
  20.7 14.9 %collective-permute-start.1 = (f32[2,128,256]{2,1,0:T(8,128)}, f32[2,128,256]{2,1,0:T(8,128)S(1)}, u32[]{:S(2)}, u32[]{:S(2)}) collective-permute-start(f32[2,128,256]{2,1,0:T(8,128)} %get-tuple-element.31), channel_id=1, source_target_pairs={{0,2},{1,3},{2,0},{3,1},{4,6},{5,7},{6,4},{7,5},{8,10},{9,11},{10,... | collective-permute-start | bytes 786440 | tf_op jit(solution)/shard_map/ppermute | solution.py:489
  23.2 21.6 %collective-permute-start.2 = (f32[2,128,256]{2,1,0:T(8,128)}, f32[2,128,256]{2,1,0:T(8,128)S(1)}, u32[]{:S(2)}, u32[]{:S(2)}) collective-permute-start(f32[2,128,256]{2,1,0:T(8,128)} %get-tuple-element.32), channel_id=1, source_target_pairs={{0,4},{1,5},{2,6},{3,7},{4,0},{5,1},{6,2},{7,3},{8,12},{9,13},{10,... | collective-permute-start | bytes 786440 | tf_op jit(solution)/shard_map/ppermute | solution.py:489
  25.8 19.0 %collective-permute-start.3 = (f32[2,128,256]{2,1,0:T(8,128)}, f32[2,128,256]{2,1,0:T(8,128)S(1)}, u32[]{:S(2)}, u32[]{:S(2)}) collective-permute-start(f32[2,128,256]{2,1,0:T(8,128)} %get-tuple-element.33), channel_id=1, source_target_pairs={{0,6},{1,7},{2,4},{3,5},{4,2},{5,3},{6,0},{7,1},{8,14},{9,15},{10,... | collective-permute-start | bytes 786440 | tf_op jit(solution)/shard_map/ppermute | solution.py:489
  35.6 9.2 %copy-start.2 = (f32[2,128,256]{2,1,0:T(8,128)}, f32[2,128,256]{2,1,0:T(8,128)S(1)}, u32[]{:S(2)}) copy-start(f32[2,128,256]{2,1,0:T(8,128)S(1)} %collective-permute-done.1.refs_1_) | copy-start | bytes 786436
  44.8 0.7 copy-start.3
  44.8 0.8 copy-start.4
  49.4 10.3 %collective-permute-start.6 = (f32[2,128,256]{2,1,0:T(8,128)}, f32[2,128,256]{2,1,0:T(8,128)S(1)}, u32[]{:S(2)}, u32[]{:S(2)}) collective-permute-start(f32[2,128,256]{2,1,0:T(8,128)} %get-tuple-element.35.refs_0_), channel_id=1, source_target_pairs={{0,24},{8,16},{16,8},{24,0},{1,25},{9,17},{17,9},{25,1},{2,26},{10... | collective-permute-start | bytes 786440 | tf_op jit(solution)/shard_map/ppermute | solution.py:495
  51.8 11.1 %collective-permute-start.5 = (f32[2,128,256]{2,1,0:T(8,128)}, f32[2,128,256]{2,1,0:T(8,128)S(1)}, u32[]{:S(2)}, u32[]{:S(2)}) collective-permute-start(f32[2,128,256]{2,1,0:T(8,128)} %get-tuple-element.35.refs_0_), channel_id=1, source_target_pairs={{0,16},{8,24},{16,0},{24,8},{1,17},{9,25},{17,1},{25,9},{2,18},{10... | collective-permute-start | bytes 786440 | tf_op jit(solution)/shard_map/ppermute | solution.py:495
  52.3 10.7 %collective-permute-start.4 = (f32[2,128,256]{2,1,0:T(8,128)}, f32[2,128,256]{2,1,0:T(8,128)S(1)}, u32[]{:S(2)}, u32[]{:S(2)}) collective-permute-start(f32[2,128,256]{2,1,0:T(8,128)} %get-tuple-element.35.refs_0_), channel_id=1, source_target_pairs={{0,8},{8,0},{16,24},{24,16},{1,9},{9,1},{17,25},{25,17},{2,10},{10... | collective-permute-start | bytes 786440 | tf_op jit(solution)/shard_map/ppermute | solution.py:495
  59.7 3.3 %copy-start.5 = (f32[2,128,256]{2,1,0:T(8,128)}, f32[2,128,256]{2,1,0:T(8,128)S(1)}, u32[]{:S(2)}) copy-start(f32[2,128,256]{2,1,0:T(8,128)S(1)} %collective-permute-done.6.refs_3_) | copy-start | bytes 786436
  62.9 0.7 copy-start.6
  63.0 0.7 copy-start.7
  67.0 11.7 %collective-permute-start.7 = (f32[2,128,128]{2,1,0:T(8,128)}, f32[2,128,128]{2,1,0:T(8,128)S(1)}, u32[]{:S(2)}, u32[]{:S(2)}) collective-permute-start(f32[2,128,128]{2,1,0:T(8,128)} %get-tuple-element.37), channel_id=1, source_target_pairs={{0,2},{1,3},{2,0},{3,1},{4,6},{5,7},{6,4},{7,5},{8,10},{9,11},{10,... | collective-permute-start | bytes 393224 | tf_op jit(solution)/shard_map/ppermute | solution.py:499
  73.1 13.1 %collective-permute-start.8 = (f32[2,128,128]{2,1,0:T(8,128)}, f32[2,128,128]{2,1,0:T(8,128)S(1)}, u32[]{:S(2)}, u32[]{:S(2)}) collective-permute-start(f32[2,128,128]{2,1,0:T(8,128)} %get-tuple-element.38), channel_id=1, source_target_pairs={{0,4},{1,5},{2,6},{3,7},{4,0},{5,1},{6,2},{7,3},{8,12},{9,13},{10,... | collective-permute-start | bytes 393224 | tf_op jit(solution)/shard_map/ppermute | solution.py:499
  74.1 12.1 %collective-permute-start.9 = (f32[2,128,128]{2,1,0:T(8,128)}, f32[2,128,128]{2,1,0:T(8,128)S(1)}, u32[]{:S(2)}, u32[]{:S(2)}) collective-permute-start(f32[2,128,128]{2,1,0:T(8,128)} %get-tuple-element.39), channel_id=1, source_target_pairs={{0,6},{1,7},{2,4},{3,5},{4,2},{5,3},{6,0},{7,1},{8,14},{9,15},{10,... | collective-permute-start | bytes 393224 | tf_op jit(solution)/shard_map/ppermute | solution.py:499
  78.7 7.5 %copy-start.8 = (f32[2,128,128]{2,1,0:T(8,128)}, f32[2,128,128]{2,1,0:T(8,128)S(1)}, u32[]{:S(2)}) copy-start(f32[2,128,128]{2,1,0:T(8,128)S(1)} %collective-permute-done.7.refs_1_) | copy-start | bytes 393220
  86.2 0.7 copy-start.9
  86.2 0.7 copy-start.10
  90.7 10.7 %collective-permute-start.10 = (f32[8,128,128]{2,1,0:T(8,128)}, f32[8,128,128]{2,1,0:T(8,128)S(1)}, u32[]{:S(2)}, u32[]{:S(2)}) collective-permute-start(f32[8,128,128]{2,1,0:T(8,128)} %get-tuple-element.40), channel_id=1, source_target_pairs={{0,1},{1,0},{2,3},{3,2},{4,5},{5,4},{6,7},{7,6},{8,9},{9,8},{10,11... | collective-permute-start | bytes 1572872 | tf_op jit(solution)/shard_map/ppermute | solution.py:502
  101.5 0.8 copy-start.1

commit v2 on v1

v2 whole, which is shorter than its diff:
```python
import functools

import jax
import jax.numpy as jnp
from jax import lax
from jax.experimental import pallas as pl
from jax.experimental.pallas import tpu as pltpu
from jax.sharding import PartitionSpec as P

ATTENTION_UNITS = 16
DK = 128
DV = 128
HALF = ATTENTION_UNITS // 2
F32 = jnp.float32
BF16 = jnp.bfloat16
HIGHEST = lax.Precision.HIGHEST
VMEM_LIMIT = 8 * 1024 * 1024
VMEM_ALL = 8 * 1024 * 1024
VECTOR = pl.BlockSpec(memory_space=pltpu.VMEM)
SCALAR = pl.BlockSpec(memory_space=pltpu.SMEM)
ANYWHERE = pl.BlockSpec(memory_space=pl.ANY)
DISTANT = pl.BlockSpec(memory_space=pltpu.HBM)


def dot(left, right):
    return jnp.dot(left, right, preferred_element_type=F32)


def dot_t(left, right):
    return lax.dot_general(left, right, (((1,), (1,)), ((), ())), preferred_element_type=F32)


def t_dot(left, right):
    return lax.dot_general(left, right, (((0,), (0,)), ((), ())), preferred_element_type=F32)


def split(x):
    high = x.astype(BF16)
    low = (x - high.astype(F32)).astype(BF16)
    return high, low


def wide(x):
    return jnp.concatenate(split(x), axis=1)


def halves_sum(x):
    width = x.shape[1] // 2
    return x[:, :width] + x[:, width:]


def mul(left, right):
    pair = wide(left)
    high, low = split(right)
    if right.shape[1] == DK:
        row = jnp.concatenate([high, low], axis=1)
        return halves_sum(dot(pair, jnp.concatenate([row, row], axis=0)))
    return dot(pair, jnp.concatenate([high, high], axis=0)) + dot(
        pair, jnp.concatenate([low, low], axis=0)
    )


def mul_exact(left, right):
    return dot(wide(left), jnp.concatenate([right, right], axis=0))


def positions(size):
    later = lax.broadcasted_iota(jnp.int32, (size, size), 0)
    earlier = lax.broadcasted_iota(jnp.int32, (size, size), 1)
    return later, earlier


def three(x):
    first = x.astype(BF16)
    rest = x - first.astype(F32)
    second = rest.astype(BF16)
    third = (rest - second.astype(F32)).astype(BF16)
    return first, second, third


def running_sum(decay_rows):
    earlier, later = positions(decay_rows.shape[1])
    ones = jnp.where(earlier <= later, 1.0, 0.0).astype(BF16)
    first, second, third = three(decay_rows)
    return dot(first, ones) + (dot(second, ones) + dot(third, ones))


def pick(x, side, start, count):
    low = x[start : start + count]
    high = x[HALF + start : HALF + start + count]
    return jnp.where(side == 0, low, high)


def lanes(ref, side, start, h):
    offset = pl.multiple_of((side * HALF + start + h) * DK, DK)
    return ref[:, pl.ds(offset, DK)]


def call(kernel, name, operands, specs, out_shape, out_specs=None, scratch=(), limit=None):
    return pl.pallas_call(
        kernel,
        out_shape=out_shape,
        in_specs=specs,
        out_specs=out_specs or jax.tree.map(lambda _: VECTOR, out_shape),
        scratch_shapes=scratch,
        compiler_params=pltpu.CompilerParams(vmem_limit_bytes=limit or VMEM_LIMIT),
        name=name,
    )(*operands)


def fetch(pairs, arrived):
    copies = [
        pltpu.make_async_copy(source, target, arrived.at[k])
        for k, (source, target) in enumerate(pairs)
    ]
    for copy in copies:
        copy.start()
    return copies


def shaped(*shape):
    return jax.ShapeDtypeStruct(shape, F32)


def staged_map_kernel(start, count, side_ref, key_ref, value_ref, decay_ref, rate_ref, *refs):
    maps_ref, inverse_ref, key_here, value_here, decay_here, rate_here, arrived = refs[-7:]
    offset = pl.multiple_of((side_ref[0] * HALF + start) * DK, DK)
    window = (slice(None), pl.ds(offset, count * DK))
    pairs = (
        (key_ref.at[window], key_here),
        (decay_ref, decay_here),
        (rate_ref, rate_here),
        (value_ref.at[window], value_here),
    )
    for copy in fetch(pairs, arrived):
        copy.wait()
    map_work(
        start,
        count,
        side_ref[0],
        [key_here[:, h * DK : (h + 1) * DK] for h in range(count)],
        [value_here[:, h * DV : (h + 1) * DV] for h in range(count)],
        decay_here[...],
        rate_here[...],
        maps_ref,
        inverse_ref,
    )


def map_kernel(start, count, side_ref, key_ref, value_ref, decay_ref, rate_ref, *refs):
    side = side_ref[0]
    map_work(
        start,
        count,
        side,
        [lanes(key_ref, side, start, h) for h in range(count)],
        [lanes(value_ref, side, start, h) for h in range(count)],
        decay_ref[...],
        rate_ref[...],
        *refs[-2:],
    )


def map_work(start, count, side, keys, values, decays, rates, maps_ref, inverse_ref):
    length = keys[0].shape[0]
    later, earlier = positions(length)
    eye = later == earlier
    strict = later > earlier
    identity = jnp.where(eye, 1.0, 0.0)
    total_row = pick(running_sum(decays), side, start, count)
    rate_row = pick(rates, side, start, count)
    total_col, rate_col = total_row.T, rate_row.T
    heads = range(count)
    grams = [dot_t(keys[h], keys[h]) for h in heads]
    lower, unit_row, unit_col = [], [], []
    for h in heads:
        diagonal = jnp.where(eye, grams[h], 0.0)
        row = lax.rsqrt(jnp.sum(diagonal, axis=0, keepdims=True) + 1e-06)
        col = lax.rsqrt(jnp.sum(diagonal, axis=1, keepdims=True) + 1e-06)
        spread = total_col[:, h : h + 1] - total_row[h : h + 1, :]
        damping = jnp.exp(jnp.where(strict, spread, 0.0))
        scale = (rate_col[:, h : h + 1] * col) * row
        lower.append(jnp.where(strict, grams[h] * scale * damping, 0.0))
        unit_row.append(row)
        unit_col.append(col)
    inverse = [
        identity - jnp.where((later // 2) == (earlier // 2), lower[h], 0.0) for h in heads
    ]
    size = 2
    while size < length:
        band = ((later // (2 * size)) == (earlier // (2 * size))) & (
            (later // size) != (earlier // size)
        )
        inner = [mul(jnp.where(band, lower[h], 0.0), inverse[h]) for h in heads]
        outer = [mul(inverse[h], inner[h]) for h in heads]
        inverse = [inverse[h] - outer[h] for h in heads]
        size *= 2
    for h in heads:
        inverse_ref[h] = inverse[h]
    for h in heads:
        row = total_row[h : h + 1, :]
        rate = rate_row[h : h + 1, :]
        erase = mul_exact(inverse[h] * (rate * jnp.exp(row) * unit_row[h]), keys[h])
        insert = mul_exact(inverse[h] * rate, values[h])
        solved = jnp.concatenate([erase, insert], axis=1)
        final = total_col[length - 1 : length, h : h + 1]
        carried = jnp.exp(final - total_col[:, h : h + 1]) * unit_col[h]
        high, low = split(solved * carried)
        moved = t_dot(keys[h], high) + t_dot(keys[h], low)
        maps_ref[h, :, :DK] = jnp.exp(final) * identity - moved[:, :DK]
        maps_ref[h, :, DK:] = moved[:, DK:]


def make_maps(side, start, count, keys, values, decays, rates, after=(), scalars=None):
    length = keys.shape[0]
    first = scalars is not None
    scratch = []
    if first:
        scratch = [
            pltpu.VMEM((length, count * DK), BF16),
            pltpu.VMEM((length, count * DV), BF16),
            pltpu.VMEM(decays.shape, F32),
            pltpu.VMEM(rates.shape, F32),
            pltpu.SemaphoreType.DMA((4,)),
        ]
    scalars = list(scalars or ())
    return call(
        functools.partial(staged_map_kernel if first else map_kernel, start, count),
        "block_maps",
        [side, keys, values, decays, rates, *scalars, *after],
        [SCALAR]
        + [DISTANT if first else VECTOR] * 4
        + [SCALAR] * len(scalars)
        + [ANYWHERE] * len(after),
        (shaped(count, DK, DK + DV), shaped(count, length, length)),
        scratch=scratch,
        limit=VMEM_ALL if first else None,
    )


def readout_kernel(start, count, side_ref, *refs):
    queries, keys, values, decays, rates, inverse = refs[:6]
    from_state, own = refs[-2:]
    side = side_ref[0]
    length = queries.shape[0]
    later, earlier = positions(length)
    within = later >= earlier
    total_row = pick(running_sum(decays[...]), side, start, count)
    rate_row = pick(rates[...], side, start, count)
    total_col = total_row.T
    for h in range(count):
        query, key, value = (lanes(ref, side, start, h) for ref in (queries, keys, values))
        wide_query = query.astype(F32)
        wide_key = key.astype(F32)
        query_unit = lax.rsqrt(jnp.sum(wide_query * wide_query, axis=1, keepdims=True) + 1e-06)
        key_unit = lax.rsqrt(jnp.sum(wide_key * wide_key, axis=1, keepdims=True) + 1e-06)
        key_row = jnp.broadcast_to(key_unit, (length, DK)).T[:1, :]
        row, rate = total_row[h : h + 1, :], rate_row[h : h + 1, :]
        damping = jnp.exp(jnp.where(within, total_col[:, h : h + 1] - row, 0.0))
        mix = jnp.where(within, dot_t(query, key) * damping * query_unit * key_row, 0.0)
        product = mul(mix, inverse[h])
        grown = jnp.exp(total_col[:, h : h + 1]) * query_unit
        erased = mul_exact(product * (rate * jnp.exp(row) * key_row), key)
        from_state[h] = grown * wide_query - erased
        own[h] = mul_exact(product * rate, value)


def make_readout(side, start, count, queries, keys, values, decays, rates, inverse, after=()):
    length = keys.shape[0]
    return call(
        functools.partial(readout_kernel, start, count),
        "readout_terms",
        [side, queries, keys, values, decays, rates, inverse, *after],
        [SCALAR] + [VECTOR] * 6 + [ANYWHERE] * len(after),
        (shaped(count, length, DK), shaped(count, length, DV)),
    )


def finish_kernel(count, block_ref, from_state_ref, own_ref, state_ref, gate_ref, gain_ref, *refs):
    out_ref = refs[-1]
    gain = gain_ref[...]
    for h in range(count):
        readout = own_ref[h] + mul(from_state_ref[h], state_ref[h])
        mean = jnp.mean(readout * readout, axis=1, keepdims=True)
        gate = gate_ref[:, h * DV : (h + 1) * DV].astype(F32)
        scaled = readout * lax.rsqrt(mean + 1e-05) * gain
        gated = scaled * (gate / (1.0 + jnp.exp(-gate)))
        out_ref[:, h * DV : (h + 1) * DV] = gated.astype(BF16)


def finish(side, start, count, from_state, own, state, gate, gain, before, after=()):
    parts = HALF // count
    block = pl.BlockSpec(
        (gate.shape[0], count * DV), lambda i, side: (0, side[0] * parts + start // count)
    )

    def whole(x):
        return pl.BlockSpec(x.shape, lambda i, where: (0,) * x.ndim)

    extra = ([] if before is None else [before]) + list(after)
    return pl.pallas_call(
        functools.partial(finish_kernel, count),
        out_shape=jax.ShapeDtypeStruct(gate.shape, BF16),
        grid_spec=pltpu.PrefetchScalarGridSpec(
            num_scalar_prefetch=1,
            grid=(1,),
            in_specs=[whole(from_state), whole(own), whole(state), block, whole(gain)]
            + [ANYWHERE] * len(extra),
            out_specs=block,
        ),
        input_output_aliases={} if before is None else {6: 0},
        compiler_params=pltpu.CompilerParams(vmem_limit_bytes=VMEM_LIMIT),
        name="gated_readout",
    )(side, from_state, own, state, gate, gain, *extra)


def compose_into(later, earlier):
    both = mul(later[:, :DK], earlier)
    return both[:, :DK], both[:, DK:] + later[:, DK:]


def chip_kernel(core_ref, z_ref, own_ref, other_ref, *refs):
    z = z_ref[0]
    count = own_ref.shape[0]
    first_out, out_refs = refs[-1 - count], refs[-count:]

    def go(first_ref, second_ref):
        for r, out_ref in enumerate(out_refs):
            a, b = compose_into(second_ref[z ^ r], first_ref[z ^ r])
            out_ref[:, :DK] = a
            out_ref[:, DK:] = b
        first_out[...] = first_ref[...]

    @pl.when(core_ref[0] == 0)
    def _():
        go(own_ref, other_ref)

    @pl.when(core_ref[0] != 0)
    def _():
        go(other_ref, own_ref)


def chip_maps(core, z, own, other, after=()):
    return call(
        chip_kernel,
        "chip_maps",
        [core, z, own, other, *after],
        [SCALAR, SCALAR, VECTOR, VECTOR] + [ANYWHERE] * len(after),
        (shaped(*own.shape),) + (shaped(DK, DK + DV),) * own.shape[0],
    )


def group_kernel(rounds, z_ref, *refs):
    z = z_ref[0]
    in_refs = refs[:rounds]
    total_ref, prefix_ref, ordered_ref = refs[-3:]
    for r in range(rounds):
        ordered_ref[z ^ r] = in_refs[r][...]
    running = ordered_ref[0]
    for k in range(1, rounds):
        prefix_ref[k - 1] = running
        a, b = compose_into(ordered_ref[k], running)
        running = jnp.concatenate([a, b], axis=1)
    total_ref[...] = running


def group_maps(z, pieces, after=()):
    rounds = len(pieces)
    return call(
        functools.partial(group_kernel, rounds),
        "group_maps",
        [z, *pieces, *after],
        [SCALAR] + [VECTOR] * rounds + [ANYWHERE] * len(after),
        (shaped(DK, DK + DV), shaped(rounds - 1, DK, DK + DV)),
        scratch=[pltpu.VMEM((rounds, DK, DK + DV), F32)],
    )


def state_kernel(
    start, count, groups, core_ref, z_ref, group_ref, initial_ref, prefix_ref, *refs
):
    z, group = z_ref[0], group_ref[0]
    ordered_ref = refs[-1]
    out_refs = refs[-1 - count : -1]
    in_refs = refs[:groups]
    for r, ref in enumerate(in_refs):
        ordered_ref[group ^ r] = ref[...]

    def advance(k, state):
        return mul(ordered_ref[k, :, :DK], state) + ordered_ref[k, :, DK:]

    state = lax.fori_loop(0, group, advance, initial_ref[core_ref[0] * HALF + start + z])
    for r, out_ref in enumerate(out_refs):
        spot = z ^ r
        back = jnp.maximum(spot - 1, 0)
        moved = mul(prefix_ref[back, :, :DK], state) + prefix_ref[back, :, DK:]
        out_ref[...] = jnp.where(spot == 0, state, moved)


def chip_states(start, count, core, z, group, initial, prefix, groups, after=()):
    return call(
        functools.partial(state_kernel, start, count, len(groups)),
        "chip_states",
        [core, z, group, initial, prefix, *groups, *after],
        [SCALAR] * 3 + [VECTOR] * (2 + len(groups)) + [ANYWHERE] * len(after),
        (shaped(DK, DV),) * count,
        scratch=[
            pltpu.VMEM((len(groups), DK, DK + DV), F32),
        ],
    )


def core_kernel(core_ref, z_ref, first_ref, *refs):
    z = z_ref[0]
    count = first_ref.shape[0]
    in_refs = refs[:count]
    keep_ref, give_ref = refs[-2:]

    def go(start_ref, later_ref):
        for r, ref in enumerate(in_refs):
            state = ref[...]
            start_ref[z ^ r] = state
            later_ref[z ^ r] = mul(first_ref[z ^ r, :, :DK], state) + first_ref[z ^ r, :, DK:]

    @pl.when(core_ref[0] == 0)
    def _():
        go(keep_ref, give_ref)

    @pl.when(core_ref[0] != 0)
    def _():
        go(give_ref, keep_ref)


def core_states(core, z, first, pieces, after=()):
    out = shaped(len(pieces), DK, DV)
    return call(
        core_kernel,
        "core_states",
        [core, z, first, *pieces, *after],
        [SCALAR] * 2 + [VECTOR] * (1 + len(pieces)) + [ANYWHERE] * len(after),
        (out, out),
    )


def matmul(left, right):
    return jnp.einsum("...ij,...jk->...ik", left, right, precision=HIGHEST)


def gathered_states(maps, initial):
    seq, grp = lax.axis_size("seq"), lax.axis_size("grp")
    place, group = lax.axis_index("seq"), lax.axis_index("grp")

    def compose(before, step):
        both = matmul(step[..., :DK], before)
        return both.at[..., DK:].add(step[..., DK:])

    heads = maps.shape[0]
    identity = jnp.concatenate(
        [jnp.eye(DK, dtype=F32), jnp.zeros((DK, DV), F32)], axis=1
    )
    identity = jnp.broadcast_to(identity, (heads, DK, DK + DV))
    everything = lax.all_gather(maps, "seq")

    def lap(k, carry):
        total, mine = carry
        mine = jnp.where(k == place, total, mine)
        return compose(total, everything[k]), mine

    total, mine = lax.fori_loop(0, seq, lap, (identity, identity))
    groups = lax.all_gather(total, "grp")

    def step(k, state):
        return matmul(groups[k][..., :DK], state) + groups[k][..., DK:]

    start = lax.fori_loop(0, group, step, initial)
    return matmul(mine[..., :DK], start) + mine[..., DK:]


def swap_pairs(size, bit):
    return [(i, i ^ bit) for i in range(size)]


def body(
    query_proj, key_proj, value_proj, log_decay, write_rate, gate_proj, norm_gain, initial_state
):
    seq, grp = lax.axis_size("seq"), lax.axis_size("grp")
    chips = seq // 2
    place = lax.axis_index("seq")
    group = lax.axis_index("grp").astype(jnp.int32).reshape(1)
    core, z = (place % 2).astype(jnp.int32).reshape(1), (place // 2).astype(jnp.int32).reshape(1)
    gain = norm_gain.reshape(1, DV)
    mine, theirs = core, 1 - core
    decays, rates = log_decay.T, write_rate.T
    fast = seq % 2 == 0 and chips in (2, 4, 8) and grp & (grp - 1) == 0

    def maps_of(side, start, count, **options):
        return make_maps(side, start, count, key_proj, value_proj, decays, rates, **options)

    def terms_of(side, start, count, inverse, after=()):
        return make_readout(
            side, start, count, query_proj, key_proj, value_proj, decays, rates, inverse, after
        )

    out = None
    if not fast:
        maps_mine, solved_mine = maps_of(mine, 0, HALF)
        maps_theirs, solved_theirs = maps_of(theirs, 0, HALF)
        maps = jnp.where(
            core[0] == 0,
            jnp.concatenate([maps_mine, maps_theirs]),
            jnp.concatenate([maps_theirs, maps_mine]),
        )
        state = gathered_states(maps, initial_state)
        for side, solved in ((mine, solved_mine), (theirs, solved_theirs)):
            part = lax.dynamic_slice_in_dim(state, side[0] * HALF, HALF)
            terms = terms_of(side, 0, HALF, solved)
            out = finish(side, 0, HALF, *terms, part, gate_proj, gain, out)
        return out

    starts = range(0, HALF, chips)
    firsts, inverses, pieces, terms, after = [], [], [], [], ()
    for k, start in enumerate(starts):
        scalars = (mine, z, group) if k == 0 else None
        maps_theirs, inverse_theirs = maps_of(theirs, start, chips, after=after, scalars=scalars)
        other = lax.ppermute(maps_theirs, "seq", swap_pairs(seq, 1))
        maps_mine, inverse_mine = maps_of(mine, start, chips, after=(inverse_theirs,))
        inverses += [(mine, start, inverse_mine), (theirs, start, inverse_theirs)]
        first, *chip = chip_maps(core, z, maps_mine, other)
        firsts.append(first)
        after = (chip[0],)
        pieces.append(
            [chip[0]]
            + [lax.ppermute(chip[r], "seq", swap_pairs(seq, 2 * r)) for r in range(1, chips)]
        )
    prefixes, groups = [], []
    for k, start in enumerate(starts):
        total, prefix = group_maps(z, pieces[k], after)
        prefixes.append(prefix)
        groups.append(
            [total] + [lax.ppermute(total, "grp", swap_pairs(grp, r)) for r in range(1, grp)]
        )
        after = (total,)
        if k == 0:
            for side, begin, inverse in inverses:
                terms.append(terms_of(side, begin, chips, inverse, after))
                after = (terms[-1][0],)
    backs = []
    for k, start in enumerate(starts):
        back = chip_states(
            start, chips, core, z, group, initial_state, prefixes[k], groups[k], after
        )
        after = (back[0],)
        backs.append(
            [back[0]]
            + [lax.ppermute(back[r], "seq", swap_pairs(seq, 2 * r)) for r in range(1, chips)]
        )
    states = []
    for k, start in enumerate(starts):
        state, give = core_states(core, z, firsts[k], backs[k], after)
        after = (state,)
        states.append((state, lax.ppermute(give, "seq", swap_pairs(seq, 1))))
    for k, start in enumerate(starts):
        for part, side in enumerate((mine, theirs)):
            out = finish(
                side, start, chips, *terms[2 * k + part], states[k][part], gate_proj, gain, out, after
            )
            after = ()
    return out


def solution(mesh):
    spread = P(("grp", "seq"), None)
    placed = (spread,) * 6 + (P(), P())
    return jax.shard_map(body, mesh=mesh, in_specs=placed, out_specs=spread, check_vma=False)
```

time: 106 us -> 70.5 us (0.67)
  waiting for transfers between devices: 39.8 us -> 7.59 us
  starting transfers between devices: 17.7 us -> 32.7 us
  Pallas kernels: 40.7 us -> 26.1 us
  local copies, waits for them, and re-layouts: 6.12 us -> 3.51 us
    ppermute x3 -> x6, waiting for transfers between devices: 19 us -> 3.3 us  [body(): lax.ppermute(chip[r], 'seq', swap_pairs(seq, 2 * r))]
    pallas_call x10 -> x20, Pallas kernels: 40.7 us -> 26.1 us  [the longest x16 22.1 us: call(): pl.pallas_call(kernel, out_shape=out_shape, in_specs=specs, out_specs=out...]
    ppermute x3 -> x6, waiting for transfers between devices: 10.2 us -> 0.02 us  [body(): lax.ppermute(total, 'grp', swap_pairs(grp, r))]
    ppermute x4 -> x8, waiting for transfers between devices: 10.6 us -> 4.26 us  [the longest x6 4.26 us: body(): lax.ppermute(back[r], 'seq', swap_pairs(seq, 2 * r))]
    ppermute x4 -> x8, starting transfers between devices: 8.53 us -> 14.6 us  [the longest x6 14.5 us: body(): lax.ppermute(back[r], 'seq', swap_pairs(seq, 2 * r))]
    ppermute x3 -> x6, starting transfers between devices: 5.16 us -> 10.1 us  [body(): lax.ppermute(chip[r], 'seq', swap_pairs(seq, 2 * r))]
    ppermute x3 -> x6, starting transfers between devices: 3.49 us -> 7.32 us  [body(): lax.ppermute(total, 'grp', swap_pairs(grp, r))]
    unnamed x28 -> x20, local copies, waits for them, and re-layouts: 6.12 us -> 3.51 us
  transfers between devices with their start and end apart: 11 -> 22, of which waited for: 7 -> 5; matrix products, arithmetic and copies ran while one was open for 1% -> 0% of each run, Pallas kernels for 16% -> 26%
where the time goes in v2:
time: 70.5 us; the launch traced here: 70.1 us
  starting transfers between devices  32.7 us (46%)
  Pallas kernels  26.1 us (37%)
  waiting for transfers between devices  7.59 us (11%)
  local copies, waits for them, and re-layouts  3.51 us (5%)
    pallas_call x16, Pallas kernels, call(): pl.pallas_call(kernel, out_shape=out_shape, in_specs=specs, out_specs=out...  22.1 us
    ppermute x6, starting transfers between devices, body(): lax.ppermute(back[r], 'seq', swap_pairs(seq, 2 * r))  14.5 us
    ppermute x6, starting transfers between devices, body(): lax.ppermute(chip[r], 'seq', swap_pairs(seq, 2 * r))  10.1 us
    ppermute x6, starting transfers between devices, body(): lax.ppermute(total, 'grp', swap_pairs(grp, r))  7.32 us
    ppermute x6, waiting for transfers between devices, body(): lax.ppermute(back[r], 'seq', swap_pairs(seq, 2 * r))  4.26 us
    pallas_call x4, Pallas kernels, finish(): pl.pallas_call(functools.partial(finish_kernel, count), out_shape=jax.Sha...  3.98 us
    unnamed x20, local copies, waits for them, and re-layouts  3.51 us
    ppermute x6, waiting for transfers between devices, body(): lax.ppermute(chip[r], 'seq', swap_pairs(seq, 2 * r))  3.3 us
  transfers between devices with their start and end apart: 22, of which 5 were waited for; matrix products, arithmetic and copies ran while one was open for 0% of the time, Pallas kernels for 26%

profile of v2, /device:TPU:0, one launch (start us, length us, event | category | flops | bytes accessed | tf_op | source)
XLA Modules:
  0.0 70.1 jit_solution(18259636358061653073)
XLA Ops:
  0.7 1.0 %copy-done = bf16[128,2048]{1,0:T(8,128)(2,1)S(1)} copy-done((bf16[128,2048]{1,0:T(8,128)(2,1)S(1)}, bf16[128,2048]{1,0:T(8,128)(2,1)}, u32[]{:S(2)}) %copy-start) | copy-done | bytes 524312
  2.8 3.5 %block_maps.4 = (f32[4,128,256]{2,1,0:T(8,128)S(1)}, f32[4,128,128]{2,1,0:T(8,128)S(1)}) custom-call(s32[1]{0:T(128)S(6)} %sub.7.side_ref.block_ref, bf16[128,2048]{1,0:T(8,128)(2,1)S(1)} %copy-done, bf16[128,2048]{1,0:T(8,128)(2,1)S(1)} %copy-done.2, f32[16,128]{1,0:T(8,128)S(1)} %bitcast.6, f32[16,128]{1,0:T(8,128)S(1)} %bitcast.14, ...), custom_call_target="tpu_custom_call" | custom-call | tf_op jit(solution)/shard_map/block_maps/pallas_call | solution.py:100
  6.8 3.4 %block_maps.5 = (f32[4,128,256]{2,1,0:T(8,128)S(1)}, f32[4,128,128]{2,1,0:T(8,128)S(1)}) custom-call(s32[1]{0:T(128)} %bitcast.refs_0_.side_ref.core_ref.block_ref, bf16[128,2048]{1,0:T(8,128)(2,1)S(1)} %copy-done.1, bf16[128,2048]{1,0:T(8,128)(2,1)S(1)} %copy-done.3, f32[16,128]{1,0:T(8,128)S(1)} %bitcast.7, f32[16,128]{1,0:T(8,128)S(1)} %bitcast.15, ...), custom_call_target="tpu_custom_call" | custom-call | tf_op jit(solution)/shard_map/block_maps/pallas_call | solution.py:100
  10.5 3.3 %block_maps.6 = (f32[4,128,256]{2,1,0:T(8,128)S(1)}, f32[4,128,128]{2,1,0:T(8,128)S(1)}) custom-call(s32[1]{0:T(128)S(6)} %sub.7.side_ref.block_ref, bf16[128,2048]{1,0:T(8,128)(2,1)S(1)} %copy-done.1, bf16[128,2048]{1,0:T(8,128)(2,1)S(1)} %copy-done.3, f32[16,128]{1,0:T(8,128)S(1)} %bitcast.8, f32[16,128]{1,0:T(8,128)S(1)} %bitcast.16, ...), custom_call_target="tpu_custom_call" | custom-call | tf_op jit(solution)/shard_map/block_maps/pallas_call | solution.py:100
  14.0 3.1 %collective-permute-start.1 = (f32[128,256]{1,0:T(8,128)S(1)}, f32[128,256]{1,0:T(8,128)S(1)}, u32[]{:S(2)}, u32[]{:S(2)}) collective-permute-start(f32[128,256]{1,0:T(8,128)S(1)} %get-tuple-element.54), channel_id=1, source_target_pairs={{0,2},{1,3},{2,0},{3,1},{4,6},{5,7},{6,4},{7,5},{8,10},{9,11},{10,... | collective-permute-start | bytes 393224 | tf_op jit(solution)/shard_map/ppermute | solution.py:533
  17.0 2.6 %collective-permute-start.2 = (f32[128,256]{1,0:T(8,128)S(1)}, f32[128,256]{1,0:T(8,128)S(1)}, u32[]{:S(2)}, u32[]{:S(2)}) collective-permute-start(f32[128,256]{1,0:T(8,128)S(1)} %get-tuple-element.55), channel_id=1, source_target_pairs={{0,4},{1,5},{2,6},{3,7},{4,0},{5,1},{6,2},{7,3},{8,12},{9,13},{10,... | collective-permute-start | bytes 393224 | tf_op jit(solution)/shard_map/ppermute | solution.py:533
  19.6 3.3 %block_maps.7 = (f32[4,128,256]{2,1,0:T(8,128)S(1)}, f32[4,128,128]{2,1,0:T(8,128)S(1)}) custom-call(s32[1]{0:T(128)} %bitcast.refs_0_.side_ref.core_ref.block_ref, bf16[128,2048]{1,0:T(8,128)(2,1)S(1)} %copy-done.1, bf16[128,2048]{1,0:T(8,128)(2,1)S(1)} %copy-done.3, f32[16,128]{1,0:T(8,128)S(1)} %bitcast.9, f32[16,128]{1,0:T(8,128)S(1)} %bitcast.17, ...), custom_call_target="tpu_custom_call" | custom-call | tf_op jit(solution)/shard_map/block_maps/pallas_call | solution.py:100
  24.5 3.5 %collective-permute-start.6 = (f32[128,256]{1,0:T(8,128)S(1)}, f32[128,256]{1,0:T(8,128)S(1)}, u32[]{:S(2)}, u32[]{:S(2)}) collective-permute-start(f32[128,256]{1,0:T(8,128)S(1)} %get-tuple-element.68), channel_id=1, source_target_pairs={{0,4},{1,5},{2,6},{3,7},{4,0},{5,1},{6,2},{7,3},{8,12},{9,13},{10,... | collective-permute-start | bytes 393224 | tf_op jit(solution)/shard_map/ppermute | solution.py:533
  28.0 2.0 %collective-permute-done.2.refs_2_ = f32[128,256]{1,0:T(8,128)S(1)} collective-permute-done((f32[128,256]{1,0:T(8,128)S(1)}, f32[128,256]{1,0:T(8,128)S(1)}, u32[]{:S(2)}, u32[]{:S(2)}) %collective-permute-start.2) | collective-permute-done | bytes 131104 | tf_op jit(solution)/shard_map/ppermute | solution.py:533
  30.6 1.6 %collective-permute-start.11 = (f32[128,256]{1,0:T(8,128)S(1)}, f32[128,256]{1,0:T(8,128)S(1)}, u32[]{:S(2)}, u32[]{:S(2)}) collective-permute-start(f32[128,256]{1,0:T(8,128)S(1)} %get-tuple-element.60.refs_6_.refs_0_), channel_id=1, source_target_pairs={{0,8},{8,0},{16,24},{24,16},{1,9},{9,1},{17,25},{25,17},{2,10},{10... | collective-permute-start | bytes 393224 | tf_op jit(solution)/shard_map/ppermute | solution.py:540
  32.2 1.5 %collective-permute-start.12 = (f32[128,256]{1,0:T(8,128)S(1)}, f32[128,256]{1,0:T(8,128)S(1)}, u32[]{:S(2)}, u32[]{:S(2)}) collective-permute-start(f32[128,256]{1,0:T(8,128)S(1)} %get-tuple-element.60.refs_6_.refs_0_), channel_id=1, source_target_pairs={{0,16},{8,24},{16,0},{24,8},{1,17},{9,25},{17,1},{25,9},{2,18},{10... | collective-permute-start | bytes 393224 | tf_op jit(solution)/shard_map/ppermute | solution.py:540
  34.4 1.4 %readout_terms.4 = (f32[4,128,128]{2,1,0:T(8,128)S(1)}, f32[4,128,128]{2,1,0:T(8,128)S(1)}) custom-call(s32[1]{0:T(128)} %bitcast.refs_0_.side_ref.core_ref.block_ref, bf16[128,2048]{1,0:T(8,128)(2,1)S(1)} %copy-done.4, bf16[128,2048]{1,0:T(8,128)(2,1)S(1)} %copy-done.1, bf16[128,2048]{1,0:T(8,128)(2,1)S(1)} %copy-done.3, f32[16,128]{1,0:T(8,128)S(1)} %bitcast.10, ...), custom_call_target="tpu_custom_call" | custom-call | tf_op jit(solution)/shard_map/readout_terms/pallas_call | solution.py:100
  35.7 1.4 %readout_terms.5 = (f32[4,128,128]{2,1,0:T(8,128)S(1)}, f32[4,128,128]{2,1,0:T(8,128)S(1)}) custom-call(s32[1]{0:T(128)S(6)} %sub.7.side_ref.block_ref, bf16[128,2048]{1,0:T(8,128)(2,1)S(1)} %copy-done.4, bf16[128,2048]{1,0:T(8,128)(2,1)S(1)} %copy-done.1, bf16[128,2048]{1,0:T(8,128)(2,1)S(1)} %copy-done.3, f32[16,128]{1,0:T(8,128)S(1)} %bitcast.11, ...), custom_call_target="tpu_custom_call" | custom-call | tf_op jit(solution)/shard_map/readout_terms/pallas_call | solution.py:100
  37.1 1.4 %readout_terms.6 = (f32[4,128,128]{2,1,0:T(8,128)S(1)}, f32[4,128,128]{2,1,0:T(8,128)S(1)}) custom-call(s32[1]{0:T(128)} %bitcast.refs_0_.side_ref.core_ref.block_ref, bf16[128,2048]{1,0:T(8,128)(2,1)S(1)} %copy-done.4, bf16[128,2048]{1,0:T(8,128)(2,1)S(1)} %copy-done.1, bf16[128,2048]{1,0:T(8,128)(2,1)S(1)} %copy-done.3, f32[16,128]{1,0:T(8,128)S(1)} %bitcast.12, ...), custom_call_target="tpu_custom_call" | custom-call | tf_op jit(solution)/shard_map/readout_terms/pallas_call | solution.py:100
  38.5 1.4 %readout_terms.7 = (f32[4,128,128]{2,1,0:T(8,128)S(1)}, f32[4,128,128]{2,1,0:T(8,128)S(1)}) custom-call(s32[1]{0:T(128)S(6)} %sub.7.side_ref.block_ref, bf16[128,2048]{1,0:T(8,128)(2,1)S(1)} %copy-done.4, bf16[128,2048]{1,0:T(8,128)(2,1)S(1)} %copy-done.1, bf16[128,2048]{1,0:T(8,128)(2,1)S(1)} %copy-done.3, f32[16,128]{1,0:T(8,128)S(1)} %bitcast.13, ...), custom_call_target="tpu_custom_call" | custom-call | tf_op jit(solution)/shard_map/readout_terms/pallas_call | solution.py:100
  39.9 1.3 %collective-permute-done.6.refs_2_ = f32[128,256]{1,0:T(8,128)S(1)} collective-permute-done((f32[128,256]{1,0:T(8,128)S(1)}, f32[128,256]{1,0:T(8,128)S(1)}, u32[]{:S(2)}, u32[]{:S(2)}) %collective-permute-start.6) | collective-permute-done | bytes 131104 | tf_op jit(solution)/shard_map/ppermute | solution.py:533
  41.8 2.5 %collective-permute-start.10 = (f32[128,256]{1,0:T(8,128)S(1)}, f32[128,256]{1,0:T(8,128)S(1)}, u32[]{:S(2)}, u32[]{:S(2)}) collective-permute-start(f32[128,256]{1,0:T(8,128)S(1)} %get-tuple-element.71.refs_4_.refs_0_), channel_id=1, source_target_pairs={{0,24},{8,16},{16,8},{24,0},{1,25},{9,17},{17,9},{25,1},{2,26},{10... | collective-permute-start | bytes 393224 | tf_op jit(solution)/shard_map/ppermute | solution.py:540
  45.7 7.6 %collective-permute-start.17 = (f32[128,128]{1,0:T(8,128)S(1)}, f32[128,128]{1,0:T(8,128)S(1)}, u32[]{:S(2)}, u32[]{:S(2)}) collective-permute-start(f32[128,128]{1,0:T(8,128)S(1)} %get-tuple-element.79), channel_id=1, source_target_pairs={{0,2},{1,3},{2,0},{3,1},{4,6},{5,7},{6,4},{7,5},{8,10},{9,11},{10,... | collective-permute-start | bytes 196616 | tf_op jit(solution)/shard_map/ppermute | solution.py:555
  54.2 1.5 %collective-permute-start.19 = (f32[128,128]{1,0:T(8,128)S(1)}, f32[128,128]{1,0:T(8,128)S(1)}, u32[]{:S(2)}, u32[]{:S(2)}) collective-permute-start(f32[128,128]{1,0:T(8,128)S(1)} %get-tuple-element.81), channel_id=1, source_target_pairs={{0,6},{1,7},{2,4},{3,5},{4,2},{5,3},{6,0},{7,1},{8,14},{9,15},{10,... | collective-permute-start | bytes 196616 | tf_op jit(solution)/shard_map/ppermute | solution.py:555
  56.0 1.7 %collective-permute-start.14 = (f32[128,128]{1,0:T(8,128)S(1)}, f32[128,128]{1,0:T(8,128)S(1)}, u32[]{:S(2)}, u32[]{:S(2)}) collective-permute-start(f32[128,128]{1,0:T(8,128)S(1)} %get-tuple-element.75), channel_id=1, source_target_pairs={{0,2},{1,3},{2,0},{3,1},{4,6},{5,7},{6,4},{7,5},{8,10},{9,11},{10,... | collective-permute-start | bytes 196616 | tf_op jit(solution)/shard_map/ppermute | solution.py:555
  57.7 1.3 %collective-permute-start.15 = (f32[128,128]{1,0:T(8,128)S(1)}, f32[128,128]{1,0:T(8,128)S(1)}, u32[]{:S(2)}, u32[]{:S(2)}) collective-permute-start(f32[128,128]{1,0:T(8,128)S(1)} %get-tuple-element.76), channel_id=1, source_target_pairs={{0,4},{1,5},{2,6},{3,7},{4,0},{5,1},{6,2},{7,3},{8,12},{9,13},{10,... | collective-permute-start | bytes 196616 | tf_op jit(solution)/shard_map/ppermute | solution.py:555
  59.0 1.5 %collective-permute-start.16 = (f32[128,128]{1,0:T(8,128)S(1)}, f32[128,128]{1,0:T(8,128)S(1)}, u32[]{:S(2)}, u32[]{:S(2)}) collective-permute-start(f32[128,128]{1,0:T(8,128)S(1)} %get-tuple-element.77), channel_id=1, source_target_pairs={{0,6},{1,7},{2,4},{3,5},{4,2},{5,3},{6,0},{7,1},{8,14},{9,15},{10,... | collective-permute-start | bytes 196616 | tf_op jit(solution)/shard_map/ppermute | solution.py:555
  61.6 2.0 %collective-permute-done.15.refs_2_ = f32[128,128]{1,0:T(8,128)S(1)} collective-permute-done((f32[128,128]{1,0:T(8,128)S(1)}, f32[128,128]{1,0:T(8,128)S(1)}, u32[]{:S(2)}, u32[]{:S(2)}) %collective-permute-start.15) | collective-permute-done | bytes 65568 | tf_op jit(solution)/shard_map/ppermute | solution.py:555
  63.6 1.5 %collective-permute-done.16.refs_3_ = f32[128,128]{1,0:T(8,128)S(1)} collective-permute-done((f32[128,128]{1,0:T(8,128)S(1)}, f32[128,128]{1,0:T(8,128)S(1)}, u32[]{:S(2)}, u32[]{:S(2)}) %collective-permute-start.16) | collective-permute-done | bytes 65568 | tf_op jit(solution)/shard_map/ppermute | solution.py:555
  (60 shorter events, 14.9 us)
Async XLA Ops:
  6.3 3.9 %collective-permute-start = (f32[4,128,256]{2,1,0:T(8,128)S(1)}, f32[4,128,256]{2,1,0:T(8,128)S(1)}, u32[]{:S(2)}, u32[]{:S(2)}) collective-permute-start(f32[4,128,256]{2,1,0:T(8,128)S(1)} %get-tuple-element.49), channel_id=1, source_target_pairs={{0,1},{1,0},{2,3},{3,2},{4,5},{5,4},{6,7},{7,6},{8,9},{9,8},{10,11... | collective-permute-start | bytes 1572872 | tf_op jit(solution)/shard_map/ppermute | solution.py:525
  13.9 9.1 %collective-permute-start.4 = (f32[4,128,256]{2,1,0:T(8,128)S(1)}, f32[4,128,256]{2,1,0:T(8,128)S(1)}, u32[]{:S(2)}, u32[]{:S(2)}) collective-permute-start(f32[4,128,256]{2,1,0:T(8,128)S(1)} %get-tuple-element.58), channel_id=1, source_target_pairs={{0,1},{1,0},{2,3},{3,2},{4,5},{5,4},{6,7},{7,6},{8,9},{9,8},{10,11... | collective-permute-start | bytes 1572872 | tf_op jit(solution)/shard_map/ppermute | solution.py:525
  14.0 14.0 %collective-permute-start.1 = (f32[128,256]{1,0:T(8,128)S(1)}, f32[128,256]{1,0:T(8,128)S(1)}, u32[]{:S(2)}, u32[]{:S(2)}) collective-permute-start(f32[128,256]{1,0:T(8,128)S(1)} %get-tuple-element.54), channel_id=1, source_target_pairs={{0,2},{1,3},{2,0},{3,1},{4,6},{5,7},{6,4},{7,5},{8,10},{9,11},{10,... | collective-permute-start | bytes 393224 | tf_op jit(solution)/shard_map/ppermute | solution.py:533
  17.0 12.9 %collective-permute-start.2 = (f32[128,256]{1,0:T(8,128)S(1)}, f32[128,256]{1,0:T(8,128)S(1)}, u32[]{:S(2)}, u32[]{:S(2)}) collective-permute-start(f32[128,256]{1,0:T(8,128)S(1)} %get-tuple-element.55), channel_id=1, source_target_pairs={{0,4},{1,5},{2,6},{3,7},{4,0},{5,1},{6,2},{7,3},{8,12},{9,13},{10,... | collective-permute-start | bytes 393224 | tf_op jit(solution)/shard_map/ppermute | solution.py:533
  19.6 10.3 %collective-permute-start.3 = (f32[128,256]{1,0:T(8,128)S(1)}, f32[128,256]{1,0:T(8,128)S(1)}, u32[]{:S(2)}, u32[]{:S(2)}) collective-permute-start(f32[128,256]{1,0:T(8,128)S(1)} %get-tuple-element.56), channel_id=1, source_target_pairs={{0,6},{1,7},{2,4},{3,5},{4,2},{5,3},{6,0},{7,1},{8,14},{9,15},{10,... | collective-permute-start | bytes 393224 | tf_op jit(solution)/shard_map/ppermute | solution.py:533
  23.5 10.9 %copy-start.4 = (bf16[128,2048]{1,0:T(8,128)(2,1)S(1)}, bf16[128,2048]{1,0:T(8,128)(2,1)}, u32[]{:S(2)}) copy-start(bf16[128,2048]{1,0:T(8,128)(2,1)} %refs_0_.7) | copy-start | bytes 1572868
  23.5 10.2 %collective-permute-start.5 = (f32[128,256]{1,0:T(8,128)S(1)}, f32[128,256]{1,0:T(8,128)S(1)}, u32[]{:S(2)}, u32[]{:S(2)}) collective-permute-start(f32[128,256]{1,0:T(8,128)S(1)} %get-tuple-element.67), channel_id=1, source_target_pairs={{0,2},{1,3},{2,0},{3,1},{4,6},{5,7},{6,4},{7,5},{8,10},{9,11},{10,... | collective-permute-start | bytes 393224 | tf_op jit(solution)/shard_map/ppermute | solution.py:533
  24.5 16.7 %collective-permute-start.6 = (f32[128,256]{1,0:T(8,128)S(1)}, f32[128,256]{1,0:T(8,128)S(1)}, u32[]{:S(2)}, u32[]{:S(2)}) collective-permute-start(f32[128,256]{1,0:T(8,128)S(1)} %get-tuple-element.68), channel_id=1, source_target_pairs={{0,4},{1,5},{2,6},{3,7},{4,0},{5,1},{6,2},{7,3},{8,12},{9,13},{10,... | collective-permute-start | bytes 393224 | tf_op jit(solution)/shard_map/ppermute | solution.py:533
  28.0 13.2 %collective-permute-start.7 = (f32[128,256]{1,0:T(8,128)S(1)}, f32[128,256]{1,0:T(8,128)S(1)}, u32[]{:S(2)}, u32[]{:S(2)}) collective-permute-start(f32[128,256]{1,0:T(8,128)S(1)} %get-tuple-element.69), channel_id=1, source_target_pairs={{0,6},{1,7},{2,4},{3,5},{4,2},{5,3},{6,0},{7,1},{8,14},{9,15},{10,... | collective-permute-start | bytes 393224 | tf_op jit(solution)/shard_map/ppermute | solution.py:533
  30.6 14.3 %collective-permute-start.11 = (f32[128,256]{1,0:T(8,128)S(1)}, f32[128,256]{1,0:T(8,128)S(1)}, u32[]{:S(2)}, u32[]{:S(2)}) collective-permute-start(f32[128,256]{1,0:T(8,128)S(1)} %get-tuple-element.60.refs_6_.refs_0_), channel_id=1, source_target_pairs={{0,8},{8,0},{16,24},{24,16},{1,9},{9,1},{17,25},{25,17},{2,10},{10... | collective-permute-start | bytes 393224 | tf_op jit(solution)/shard_map/ppermute | solution.py:540
  32.2 13.2 %collective-permute-start.12 = (f32[128,256]{1,0:T(8,128)S(1)}, f32[128,256]{1,0:T(8,128)S(1)}, u32[]{:S(2)}, u32[]{:S(2)}) collective-permute-start(f32[128,256]{1,0:T(8,128)S(1)} %get-tuple-element.60.refs_6_.refs_0_), channel_id=1, source_target_pairs={{0,16},{8,24},{16,0},{24,8},{1,17},{9,25},{17,1},{25,9},{2,18},{10... | collective-permute-start | bytes 393224 | tf_op jit(solution)/shard_map/ppermute | solution.py:540
  33.7 11.7 %collective-permute-start.13 = (f32[128,256]{1,0:T(8,128)S(1)}, f32[128,256]{1,0:T(8,128)S(1)}, u32[]{:S(2)}, u32[]{:S(2)}) collective-permute-start(f32[128,256]{1,0:T(8,128)S(1)} %get-tuple-element.60.refs_6_.refs_0_), channel_id=1, source_target_pairs={{0,24},{8,16},{16,8},{24,0},{1,25},{9,17},{17,9},{25,1},{2,26},{10... | collective-permute-start | bytes 393224 | tf_op jit(solution)/shard_map/ppermute | solution.py:540
  38.5 6.9 %copy-start.6 = (f32[16,128,128]{2,1,0:T(8,128)S(1)}, f32[16,128,128]{2,1,0:T(8,128)}, u32[]{:S(2)}) copy-start(f32[16,128,128]{2,1,0:T(8,128)} %initial_ref.3) | copy-start | bytes 3145732
  41.8 12.4 %collective-permute-start.10 = (f32[128,256]{1,0:T(8,128)S(1)}, f32[128,256]{1,0:T(8,128)S(1)}, u32[]{:S(2)}, u32[]{:S(2)}) collective-permute-start(f32[128,256]{1,0:T(8,128)S(1)} %get-tuple-element.71.refs_4_.refs_0_), channel_id=1, source_target_pairs={{0,24},{8,16},{16,8},{24,0},{1,25},{9,17},{17,9},{25,1},{2,26},{10... | collective-permute-start | bytes 393224 | tf_op jit(solution)/shard_map/ppermute | solution.py:540
  44.3 11.4 %collective-permute-start.8 = (f32[128,256]{1,0:T(8,128)S(1)}, f32[128,256]{1,0:T(8,128)S(1)}, u32[]{:S(2)}, u32[]{:S(2)}) collective-permute-start(f32[128,256]{1,0:T(8,128)S(1)} %get-tuple-element.71.refs_4_.refs_0_), channel_id=1, source_target_pairs={{0,8},{8,0},{16,24},{24,16},{1,9},{9,1},{17,25},{25,17},{2,10},{10... | collective-permute-start | bytes 393224 | tf_op jit(solution)/shard_map/ppermute | solution.py:540
  44.9 10.8 %collective-permute-start.9 = (f32[128,256]{1,0:T(8,128)S(1)}, f32[128,256]{1,0:T(8,128)S(1)}, u32[]{:S(2)}, u32[]{:S(2)}) collective-permute-start(f32[128,256]{1,0:T(8,128)S(1)} %get-tuple-element.71.refs_4_.refs_0_), channel_id=1, source_target_pairs={{0,16},{8,24},{16,0},{24,8},{1,17},{9,25},{17,1},{25,9},{2,18},{10... | collective-permute-start | bytes 393224 | tf_op jit(solution)/shard_map/ppermute | solution.py:540
  45.7 13.3 %collective-permute-start.17 = (f32[128,128]{1,0:T(8,128)S(1)}, f32[128,128]{1,0:T(8,128)S(1)}, u32[]{:S(2)}, u32[]{:S(2)}) collective-permute-start(f32[128,128]{1,0:T(8,128)S(1)} %get-tuple-element.79), channel_id=1, source_target_pairs={{0,2},{1,3},{2,0},{3,1},{4,6},{5,7},{6,4},{7,5},{8,10},{9,11},{10,... | collective-permute-start | bytes 196616 | tf_op jit(solution)/shard_map/ppermute | solution.py:555
  53.3 7.9 %collective-permute-start.18 = (f32[128,128]{1,0:T(8,128)S(1)}, f32[128,128]{1,0:T(8,128)S(1)}, u32[]{:S(2)}, u32[]{:S(2)}) collective-permute-start(f32[128,128]{1,0:T(8,128)S(1)} %get-tuple-element.80), channel_id=1, source_target_pairs={{0,4},{1,5},{2,6},{3,7},{4,0},{5,1},{6,2},{7,3},{8,12},{9,13},{10,... | collective-permute-start | bytes 196616 | tf_op jit(solution)/shard_map/ppermute | solution.py:555
  54.2 7.0 %collective-permute-start.19 = (f32[128,128]{1,0:T(8,128)S(1)}, f32[128,128]{1,0:T(8,128)S(1)}, u32[]{:S(2)}, u32[]{:S(2)}) collective-permute-start(f32[128,128]{1,0:T(8,128)S(1)} %get-tuple-element.81), channel_id=1, source_target_pairs={{0,6},{1,7},{2,4},{3,5},{4,2},{5,3},{6,0},{7,1},{8,14},{9,15},{10,... | collective-permute-start | bytes 196616 | tf_op jit(solution)/shard_map/ppermute | solution.py:555
  56.0 5.6 %collective-permute-start.14 = (f32[128,128]{1,0:T(8,128)S(1)}, f32[128,128]{1,0:T(8,128)S(1)}, u32[]{:S(2)}, u32[]{:S(2)}) collective-permute-start(f32[128,128]{1,0:T(8,128)S(1)} %get-tuple-element.75), channel_id=1, source_target_pairs={{0,2},{1,3},{2,0},{3,1},{4,6},{5,7},{6,4},{7,5},{8,10},{9,11},{10,... | collective-permute-start | bytes 196616 | tf_op jit(solution)/shard_map/ppermute | solution.py:555
  57.7 5.9 %collective-permute-start.15 = (f32[128,128]{1,0:T(8,128)S(1)}, f32[128,128]{1,0:T(8,128)S(1)}, u32[]{:S(2)}, u32[]{:S(2)}) collective-permute-start(f32[128,128]{1,0:T(8,128)S(1)} %get-tuple-element.76), channel_id=1, source_target_pairs={{0,4},{1,5},{2,6},{3,7},{4,0},{5,1},{6,2},{7,3},{8,12},{9,13},{10,... | collective-permute-start | bytes 196616 | tf_op jit(solution)/shard_map/ppermute | solution.py:555
  59.0 6.1 %collective-permute-start.16 = (f32[128,128]{1,0:T(8,128)S(1)}, f32[128,128]{1,0:T(8,128)S(1)}, u32[]{:S(2)}, u32[]{:S(2)}) collective-permute-start(f32[128,128]{1,0:T(8,128)S(1)} %get-tuple-element.77), channel_id=1, source_target_pairs={{0,6},{1,7},{2,4},{3,5},{4,2},{5,3},{6,0},{7,1},{8,14},{9,15},{10,... | collective-permute-start | bytes 196616 | tf_op jit(solution)/shard_map/ppermute | solution.py:555
  61.5 5.6 %collective-permute-start.21 = (f32[4,128,128]{2,1,0:T(8,128)S(1)}, f32[4,128,128]{2,1,0:T(8,128)S(1)}, u32[]{:S(2)}, u32[]{:S(2)}) collective-permute-start(f32[4,128,128]{2,1,0:T(8,128)S(1)} %get-tuple-element.87), channel_id=1, source_target_pairs={{0,1},{1,0},{2,3},{3,2},{4,5},{5,4},{6,7},{7,6},{8,9},{9,8},{10,11... | collective-permute-start | bytes 786440 | tf_op jit(solution)/shard_map/ppermute | solution.py:561
  65.3 3.8 %collective-permute-start.20 = (f32[4,128,128]{2,1,0:T(8,128)S(1)}, f32[4,128,128]{2,1,0:T(8,128)S(1)}, u32[]{:S(2)}, u32[]{:S(2)}) collective-permute-start(f32[4,128,128]{2,1,0:T(8,128)S(1)} %get-tuple-element.83), channel_id=1, source_target_pairs={{0,1},{1,0},{2,3},{3,2},{4,5},{5,4},{6,7},{7,6},{8,9},{9,8},{10,11... | collective-permute-start | bytes 786440 | tf_op jit(solution)/shard_map/ppermute | solution.py:561
  (8 other events, 13.3 us)

commit v3 on v2

--- a/solution.py
+++ b/solution.py
@@ -132,14 +132,21 @@
         (rate_ref, rate_here),
         (value_ref.at[window], value_here),
     )
-    for copy in fetch(pairs, arrived):
-        copy.wait()
+    key_copy, decay_copy, rate_copy, value_copy = fetch(pairs, arrived)
+    decay_copy.wait()
+    rate_copy.wait()
+    key_copy.wait()
+
+    def values():
+        value_copy.wait()
+        return [value_here[:, h * DV : (h + 1) * DV] for h in range(count)]
+
     map_work(
         start,
         count,
         side_ref[0],
         [key_here[:, h * DK : (h + 1) * DK] for h in range(count)],
-        [value_here[:, h * DV : (h + 1) * DV] for h in range(count)],
+        values,
         decay_here[...],
         rate_here[...],
         maps_ref,
@@ -154,7 +161,7 @@
         count,
         side,
         [lanes(key_ref, side, start, h) for h in range(count)],
-        [lanes(value_ref, side, start, h) for h in range(count)],
+        lambda: [lanes(value_ref, side, start, h) for h in range(count)],
         decay_ref[...],
         rate_ref[...],
         *refs[-2:],
@@ -197,6 +204,7 @@
         size *= 2
     for h in heads:
         inverse_ref[h] = inverse[h]
+    values = values()
     for h in heads:
         row = total_row[h : h + 1, :]
         rate = rate_row[h : h + 1, :]
@@ -223,6 +231,7 @@
             pltpu.VMEM(rates.shape, F32),
             pltpu.SemaphoreType.DMA((4,)),
         ]
+        keys, values = (pltpu.with_memory_space_constraint(x, pltpu.HBM) for x in (keys, values))
     scalars = list(scalars or ())
     return call(
         functools.partial(staged_map_kernel if first else map_kernel, start, count),
@@ -554,17 +563,14 @@
             [back[0]]
             + [lax.ppermute(back[r], "seq", swap_pairs(seq, 2 * r)) for r in range(1, chips)]
         )
-    states = []
     for k, start in enumerate(starts):
         state, give = core_states(core, z, firsts[k], backs[k], after)
-        after = (state,)
-        states.append((state, lax.ppermute(give, "seq", swap_pairs(seq, 1))))
-    for k, start in enumerate(starts):
+        states = (state, lax.ppermute(give, "seq", swap_pairs(seq, 1)))
         for part, side in enumerate((mine, theirs)):
             out = finish(
-                side, start, chips, *terms[2 * k + part], states[k][part], gate_proj, gain, out, after
+                side, start, chips, *terms[2 * k + part], states[part], gate_proj, gain, out
             )
-            after = ()
+        after = (pltpu.with_memory_space_constraint(out, pltpu.HBM),)
     return out
 
 

time: 70.5 us -> 73.5 us (1.043)
  waiting for transfers between devices: 7.59 us -> 10.7 us
  local copies, waits for them, and re-layouts: 3.51 us -> 1.39 us
  Pallas kernels: 26.1 us -> 27.3 us
  starting transfers between devices: 32.7 us -> 33.6 us
    ppermute x6, waiting for transfers between devices: 4.26 us -> 6.74 us  [body(): lax.ppermute(back[r], 'seq', swap_pairs(seq, 2 * r))]
    unnamed x20 -> x16, local copies, waits for them, and re-layouts: 3.51 us -> 1.39 us
    pallas_call x16, Pallas kernels: 22.1 us -> 23.3 us  [call(): pl.pallas_call(kernel, out_shape=out_shape, in_specs=specs, out_specs=out...]
    ppermute x6, starting transfers between devices: 14.5 us -> 15.6 us  [body(): lax.ppermute(back[r], 'seq', swap_pairs(seq, 2 * r))]
  transfers between devices with their start and end apart: 22 -> 22, of which waited for: 5 -> 6; matrix products, arithmetic and copies ran while one was open for 0% -> 0% of each run, Pallas kernels for 26% -> 24%
where the time goes in v3:
time: 73.5 us; the launch traced here: 73.3 us
  starting transfers between devices  33.6 us (46%)
  Pallas kernels  27.3 us (37%)
  waiting for transfers between devices  10.7 us (15%)
  local copies, waits for them, and re-layouts  1.39 us (2%)
    pallas_call x16, Pallas kernels, call(): pl.pallas_call(kernel, out_shape=out_shape, in_specs=specs, out_specs=out...  23.3 us
    ppermute x6, starting transfers between devices, body(): lax.ppermute(back[r], 'seq', swap_pairs(seq, 2 * r))  15.6 us
    ppermute x6, starting transfers between devices, body(): lax.ppermute(chip[r], 'seq', swap_pairs(seq, 2 * r))  10.1 us
    ppermute x6, starting transfers between devices, body(): lax.ppermute(total, 'grp', swap_pairs(grp, r))  7.17 us
    ppermute x6, waiting for transfers between devices, body(): lax.ppermute(back[r], 'seq', swap_pairs(seq, 2 * r))  6.74 us
    pallas_call x4, Pallas kernels, finish(): pl.pallas_call(functools.partial(finish_kernel, count), out_shape=jax.Sha...  3.99 us
    ppermute x6, waiting for transfers between devices, body(): lax.ppermute(chip[r], 'seq', swap_pairs(seq, 2 * r))  3.46 us
  transfers between devices with their start and end apart: 22, of which 6 were waited for; matrix products, arithmetic and copies ran while one was open for 0% of the time, Pallas kernels for 24%

profile of v3, /device:TPU:0, one launch (start us, length us, event | category | flops | bytes accessed | tf_op | source)
XLA Modules:
  0.0 73.3 jit_solution(14511339722868647218)
XLA Ops:
  0.7 4.6 %block_maps.4 = (f32[4,128,256]{2,1,0:T(8,128)S(1)}, f32[4,128,128]{2,1,0:T(8,128)S(1)}) custom-call(s32[1]{0:T(128)S(6)} %sub.7.side_ref.block_ref, bf16[128,2048]{1,0:T(8,128)(2,1)} %refs_1_.7, bf16[128,2048]{1,0:T(8,128)(2,1)} %refs_2_.7, f32[16,128]{1,0:T(8,128)S(1)} %bitcast.6, f32[16,128]{1,0:T(8,128)S(1)} %bitcast.14, ...), custom_call_target="tpu_custom_call" | custom-call | tf_op jit(solution)/shard_map/block_maps/pallas_call | solution.py:100
  5.9 3.4 %block_maps.5 = (f32[4,128,256]{2,1,0:T(8,128)S(1)}, f32[4,128,128]{2,1,0:T(8,128)S(1)}) custom-call(s32[1]{0:T(128)} %bitcast.refs_0_.side_ref.core_ref.block_ref, bf16[128,2048]{1,0:T(8,128)(2,1)S(1)} %copy-done, bf16[128,2048]{1,0:T(8,128)(2,1)S(1)} %copy-done.1, f32[16,128]{1,0:T(8,128)S(1)} %bitcast.7, f32[16,128]{1,0:T(8,128)S(1)} %bitcast.15, ...), custom_call_target="tpu_custom_call" | custom-call | tf_op jit(solution)/shard_map/block_maps/pallas_call | solution.py:100
  9.6 3.3 %block_maps.6 = (f32[4,128,256]{2,1,0:T(8,128)S(1)}, f32[4,128,128]{2,1,0:T(8,128)S(1)}) custom-call(s32[1]{0:T(128)S(6)} %sub.7.side_ref.block_ref, bf16[128,2048]{1,0:T(8,128)(2,1)S(1)} %copy-done, bf16[128,2048]{1,0:T(8,128)(2,1)S(1)} %copy-done.1, f32[16,128]{1,0:T(8,128)S(1)} %bitcast.8, f32[16,128]{1,0:T(8,128)S(1)} %bitcast.16, ...), custom_call_target="tpu_custom_call" | custom-call | tf_op jit(solution)/shard_map/block_maps/pallas_call | solution.py:100
  13.1 3.0 %collective-permute-start.1 = (f32[128,256]{1,0:T(8,128)S(1)}, f32[128,256]{1,0:T(8,128)S(1)}, u32[]{:S(2)}, u32[]{:S(2)}) collective-permute-start(f32[128,256]{1,0:T(8,128)S(1)} %get-tuple-element.54), channel_id=1, source_target_pairs={{0,2},{1,3},{2,0},{3,1},{4,6},{5,7},{6,4},{7,5},{8,10},{9,11},{10,... | collective-permute-start | bytes 393224 | tf_op jit(solution)/shard_map/ppermute | solution.py:542
  16.1 2.6 %collective-permute-start.2 = (f32[128,256]{1,0:T(8,128)S(1)}, f32[128,256]{1,0:T(8,128)S(1)}, u32[]{:S(2)}, u32[]{:S(2)}) collective-permute-start(f32[128,256]{1,0:T(8,128)S(1)} %get-tuple-element.55), channel_id=1, source_target_pairs={{0,4},{1,5},{2,6},{3,7},{4,0},{5,1},{6,2},{7,3},{8,12},{9,13},{10,... | collective-permute-start | bytes 393224 | tf_op jit(solution)/shard_map/ppermute | solution.py:542
  18.7 3.3 %block_maps.7 = (f32[4,128,256]{2,1,0:T(8,128)S(1)}, f32[4,128,128]{2,1,0:T(8,128)S(1)}) custom-call(s32[1]{0:T(128)} %bitcast.refs_0_.side_ref.core_ref.block_ref, bf16[128,2048]{1,0:T(8,128)(2,1)S(1)} %copy-done, bf16[128,2048]{1,0:T(8,128)(2,1)S(1)} %copy-done.1, f32[16,128]{1,0:T(8,128)S(1)} %bitcast.9, f32[16,128]{1,0:T(8,128)S(1)} %bitcast.17, ...), custom_call_target="tpu_custom_call" | custom-call | tf_op jit(solution)/shard_map/block_maps/pallas_call | solution.py:100
  23.5 3.5 %collective-permute-start.6 = (f32[128,256]{1,0:T(8,128)S(1)}, f32[128,256]{1,0:T(8,128)S(1)}, u32[]{:S(2)}, u32[]{:S(2)}) collective-permute-start(f32[128,256]{1,0:T(8,128)S(1)} %get-tuple-element.68), channel_id=1, source_target_pairs={{0,4},{1,5},{2,6},{3,7},{4,0},{5,1},{6,2},{7,3},{8,12},{9,13},{10,... | collective-permute-start | bytes 393224 | tf_op jit(solution)/shard_map/ppermute | solution.py:542
  27.0 2.0 %collective-permute-done.2.refs_2_ = f32[128,256]{1,0:T(8,128)S(1)} collective-permute-done((f32[128,256]{1,0:T(8,128)S(1)}, f32[128,256]{1,0:T(8,128)S(1)}, u32[]{:S(2)}, u32[]{:S(2)}) %collective-permute-start.2) | collective-permute-done | bytes 131104 | tf_op jit(solution)/shard_map/ppermute | solution.py:542
  29.7 1.5 %collective-permute-start.11 = (f32[128,256]{1,0:T(8,128)S(1)}, f32[128,256]{1,0:T(8,128)S(1)}, u32[]{:S(2)}, u32[]{:S(2)}) collective-permute-start(f32[128,256]{1,0:T(8,128)S(1)} %get-tuple-element.60.refs_6_.refs_0_), channel_id=1, source_target_pairs={{0,8},{8,0},{16,24},{24,16},{1,9},{9,1},{17,25},{25,17},{2,10},{10... | collective-permute-start | bytes 393224 | tf_op jit(solution)/shard_map/ppermute | solution.py:549
  31.2 1.5 %collective-permute-start.12 = (f32[128,256]{1,0:T(8,128)S(1)}, f32[128,256]{1,0:T(8,128)S(1)}, u32[]{:S(2)}, u32[]{:S(2)}) collective-permute-start(f32[128,256]{1,0:T(8,128)S(1)} %get-tuple-element.60.refs_6_.refs_0_), channel_id=1, source_target_pairs={{0,16},{8,24},{16,0},{24,8},{1,17},{9,25},{17,1},{25,9},{2,18},{10... | collective-permute-start | bytes 393224 | tf_op jit(solution)/shard_map/ppermute | solution.py:549
  32.7 1.4 %readout_terms.4 = (f32[4,128,128]{2,1,0:T(8,128)S(1)}, f32[4,128,128]{2,1,0:T(8,128)S(1)}) custom-call(s32[1]{0:T(128)} %bitcast.refs_0_.side_ref.core_ref.block_ref, bf16[128,2048]{1,0:T(8,128)(2,1)S(1)} %copy-done.2, bf16[128,2048]{1,0:T(8,128)(2,1)S(1)} %copy-done, bf16[128,2048]{1,0:T(8,128)(2,1)S(1)} %copy-done.1, f32[16,128]{1,0:T(8,128)S(1)} %bitcast.10, ...), custom_call_target="tpu_custom_call" | custom-call | tf_op jit(solution)/shard_map/readout_terms/pallas_call | solution.py:100
  34.1 1.4 %readout_terms.5 = (f32[4,128,128]{2,1,0:T(8,128)S(1)}, f32[4,128,128]{2,1,0:T(8,128)S(1)}) custom-call(s32[1]{0:T(128)S(6)} %sub.7.side_ref.block_ref, bf16[128,2048]{1,0:T(8,128)(2,1)S(1)} %copy-done.2, bf16[128,2048]{1,0:T(8,128)(2,1)S(1)} %copy-done, bf16[128,2048]{1,0:T(8,128)(2,1)S(1)} %copy-done.1, f32[16,128]{1,0:T(8,128)S(1)} %bitcast.11, ...), custom_call_target="tpu_custom_call" | custom-call | tf_op jit(solution)/shard_map/readout_terms/pallas_call | solution.py:100
  35.5 1.4 %readout_terms.6 = (f32[4,128,128]{2,1,0:T(8,128)S(1)}, f32[4,128,128]{2,1,0:T(8,128)S(1)}) custom-call(s32[1]{0:T(128)} %bitcast.refs_0_.side_ref.core_ref.block_ref, bf16[128,2048]{1,0:T(8,128)(2,1)S(1)} %copy-done.2, bf16[128,2048]{1,0:T(8,128)(2,1)S(1)} %copy-done, bf16[128,2048]{1,0:T(8,128)(2,1)S(1)} %copy-done.1, f32[16,128]{1,0:T(8,128)S(1)} %bitcast.12, ...), custom_call_target="tpu_custom_call" | custom-call | tf_op jit(solution)/shard_map/readout_terms/pallas_call | solution.py:100
  37.4 1.4 %readout_terms.7 = (f32[4,128,128]{2,1,0:T(8,128)S(1)}, f32[4,128,128]{2,1,0:T(8,128)S(1)}) custom-call(s32[1]{0:T(128)S(6)} %sub.7.side_ref.block_ref, bf16[128,2048]{1,0:T(8,128)(2,1)S(1)} %copy-done.2, bf16[128,2048]{1,0:T(8,128)(2,1)S(1)} %copy-done, bf16[128,2048]{1,0:T(8,128)(2,1)S(1)} %copy-done.1, f32[16,128]{1,0:T(8,128)S(1)} %bitcast.13, ...), custom_call_target="tpu_custom_call" | custom-call | tf_op jit(solution)/shard_map/readout_terms/pallas_call | solution.py:100
  38.8 1.4 %collective-permute-done.6.refs_2_ = f32[128,256]{1,0:T(8,128)S(1)} collective-permute-done((f32[128,256]{1,0:T(8,128)S(1)}, f32[128,256]{1,0:T(8,128)S(1)}, u32[]{:S(2)}, u32[]{:S(2)}) %collective-permute-start.6) | collective-permute-done | bytes 131104 | tf_op jit(solution)/shard_map/ppermute | solution.py:542
  40.9 2.5 %collective-permute-start.10 = (f32[128,256]{1,0:T(8,128)S(1)}, f32[128,256]{1,0:T(8,128)S(1)}, u32[]{:S(2)}, u32[]{:S(2)}) collective-permute-start(f32[128,256]{1,0:T(8,128)S(1)} %get-tuple-element.71.refs_4_.refs_0_), channel_id=1, source_target_pairs={{0,24},{8,16},{16,8},{24,0},{1,25},{9,17},{17,9},{25,1},{2,26},{10... | collective-permute-start | bytes 393224 | tf_op jit(solution)/shard_map/ppermute | solution.py:549
  44.8 7.6 %collective-permute-start.17 = (f32[128,128]{1,0:T(8,128)S(1)}, f32[128,128]{1,0:T(8,128)S(1)}, u32[]{:S(2)}, u32[]{:S(2)}) collective-permute-start(f32[128,128]{1,0:T(8,128)S(1)} %get-tuple-element.80), channel_id=1, source_target_pairs={{0,2},{1,3},{2,0},{3,1},{4,6},{5,7},{6,4},{7,5},{8,10},{9,11},{10,... | collective-permute-start | bytes 196616 | tf_op jit(solution)/shard_map/ppermute | solution.py:564
  52.4 2.1 %collective-permute-start.18 = (f32[128,128]{1,0:T(8,128)S(1)}, f32[128,128]{1,0:T(8,128)S(1)}, u32[]{:S(2)}, u32[]{:S(2)}) collective-permute-start(f32[128,128]{1,0:T(8,128)S(1)} %get-tuple-element.81), channel_id=1, source_target_pairs={{0,4},{1,5},{2,6},{3,7},{4,0},{5,1},{6,2},{7,3},{8,12},{9,13},{10,... | collective-permute-start | bytes 196616 | tf_op jit(solution)/shard_map/ppermute | solution.py:564
  54.5 1.4 %collective-permute-start.19 = (f32[128,128]{1,0:T(8,128)S(1)}, f32[128,128]{1,0:T(8,128)S(1)}, u32[]{:S(2)}, u32[]{:S(2)}) collective-permute-start(f32[128,128]{1,0:T(8,128)S(1)} %get-tuple-element.82), channel_id=1, source_target_pairs={{0,6},{1,7},{2,4},{3,5},{4,2},{5,3},{6,0},{7,1},{8,14},{9,15},{10,... | collective-permute-start | bytes 196616 | tf_op jit(solution)/shard_map/ppermute | solution.py:564
  56.2 1.3 %collective-permute-done.18.refs_2_ = f32[128,128]{1,0:T(8,128)S(1)} collective-permute-done((f32[128,128]{1,0:T(8,128)S(1)}, f32[128,128]{1,0:T(8,128)S(1)}, u32[]{:S(2)}, u32[]{:S(2)}) %collective-permute-start.18) | collective-permute-done | bytes 65568 | tf_op jit(solution)/shard_map/ppermute | solution.py:564
  57.6 3.1 %collective-permute-done.19.refs_3_ = f32[128,128]{1,0:T(8,128)S(1)} collective-permute-done((f32[128,128]{1,0:T(8,128)S(1)}, f32[128,128]{1,0:T(8,128)S(1)}, u32[]{:S(2)}, u32[]{:S(2)}) %collective-permute-start.19) | collective-permute-done | bytes 65568 | tf_op jit(solution)/shard_map/ppermute | solution.py:564
  61.9 1.2 %collective-permute-start.15 = (f32[128,128]{1,0:T(8,128)S(1)}, f32[128,128]{1,0:T(8,128)S(1)}, u32[]{:S(2)}, u32[]{:S(2)}) collective-permute-start(f32[128,128]{1,0:T(8,128)S(1)} %get-tuple-element.76), channel_id=1, source_target_pairs={{0,4},{1,5},{2,6},{3,7},{4,0},{5,1},{6,2},{7,3},{8,12},{9,13},{10,... | collective-permute-start | bytes 196616 | tf_op jit(solution)/shard_map/ppermute | solution.py:564
  63.1 2.4 %collective-permute-start.16 = (f32[128,128]{1,0:T(8,128)S(1)}, f32[128,128]{1,0:T(8,128)S(1)}, u32[]{:S(2)}, u32[]{:S(2)}) collective-permute-start(f32[128,128]{1,0:T(8,128)S(1)} %get-tuple-element.77), channel_id=1, source_target_pairs={{0,6},{1,7},{2,4},{3,5},{4,2},{5,3},{6,0},{7,1},{8,14},{9,15},{10,... | collective-permute-start | bytes 196616 | tf_op jit(solution)/shard_map/ppermute | solution.py:564
  68.2 2.3 %collective-permute-done.15.refs_2_ = f32[128,128]{1,0:T(8,128)S(1)} collective-permute-done((f32[128,128]{1,0:T(8,128)S(1)}, f32[128,128]{1,0:T(8,128)S(1)}, u32[]{:S(2)}, u32[]{:S(2)}) %collective-permute-start.15) | collective-permute-done | bytes 65568 | tf_op jit(solution)/shard_map/ppermute | solution.py:564
  (56 shorter events, 13.3 us)
Async XLA Ops:
  5.3 3.9 %collective-permute-start = (f32[4,128,256]{2,1,0:T(8,128)S(1)}, f32[4,128,256]{2,1,0:T(8,128)S(1)}, u32[]{:S(2)}, u32[]{:S(2)}) collective-permute-start(f32[4,128,256]{2,1,0:T(8,128)S(1)} %get-tuple-element.49), channel_id=1, source_target_pairs={{0,1},{1,0},{2,3},{3,2},{4,5},{5,4},{6,7},{7,6},{8,9},{9,8},{10,11... | collective-permute-start | bytes 1572872 | tf_op jit(solution)/shard_map/ppermute | solution.py:534
  13.0 9.1 %collective-permute-start.4 = (f32[4,128,256]{2,1,0:T(8,128)S(1)}, f32[4,128,256]{2,1,0:T(8,128)S(1)}, u32[]{:S(2)}, u32[]{:S(2)}) collective-permute-start(f32[4,128,256]{2,1,0:T(8,128)S(1)} %get-tuple-element.58), channel_id=1, source_target_pairs={{0,1},{1,0},{2,3},{3,2},{4,5},{5,4},{6,7},{7,6},{8,9},{9,8},{10,11... | collective-permute-start | bytes 1572872 | tf_op jit(solution)/shard_map/ppermute | solution.py:534
  13.1 14.0 %collective-permute-start.1 = (f32[128,256]{1,0:T(8,128)S(1)}, f32[128,256]{1,0:T(8,128)S(1)}, u32[]{:S(2)}, u32[]{:S(2)}) collective-permute-start(f32[128,256]{1,0:T(8,128)S(1)} %get-tuple-element.54), channel_id=1, source_target_pairs={{0,2},{1,3},{2,0},{3,1},{4,6},{5,7},{6,4},{7,5},{8,10},{9,11},{10,... | collective-permute-start | bytes 393224 | tf_op jit(solution)/shard_map/ppermute | solution.py:542
  16.1 12.9 %collective-permute-start.2 = (f32[128,256]{1,0:T(8,128)S(1)}, f32[128,256]{1,0:T(8,128)S(1)}, u32[]{:S(2)}, u32[]{:S(2)}) collective-permute-start(f32[128,256]{1,0:T(8,128)S(1)} %get-tuple-element.55), channel_id=1, source_target_pairs={{0,4},{1,5},{2,6},{3,7},{4,0},{5,1},{6,2},{7,3},{8,12},{9,13},{10,... | collective-permute-start | bytes 393224 | tf_op jit(solution)/shard_map/ppermute | solution.py:542
  18.7 10.3 %collective-permute-start.3 = (f32[128,256]{1,0:T(8,128)S(1)}, f32[128,256]{1,0:T(8,128)S(1)}, u32[]{:S(2)}, u32[]{:S(2)}) collective-permute-start(f32[128,256]{1,0:T(8,128)S(1)} %get-tuple-element.56), channel_id=1, source_target_pairs={{0,6},{1,7},{2,4},{3,5},{4,2},{5,3},{6,0},{7,1},{8,14},{9,15},{10,... | collective-permute-start | bytes 393224 | tf_op jit(solution)/shard_map/ppermute | solution.py:542
  22.6 10.2 %copy-start.2 = (bf16[128,2048]{1,0:T(8,128)(2,1)S(1)}, bf16[128,2048]{1,0:T(8,128)(2,1)}, u32[]{:S(2)}) copy-start(bf16[128,2048]{1,0:T(8,128)(2,1)} %refs_0_.7) | copy-start | bytes 1572868
  22.6 14.3 %collective-permute-start.5 = (f32[128,256]{1,0:T(8,128)S(1)}, f32[128,256]{1,0:T(8,128)S(1)}, u32[]{:S(2)}, u32[]{:S(2)}) collective-permute-start(f32[128,256]{1,0:T(8,128)S(1)} %get-tuple-element.67), channel_id=1, source_target_pairs={{0,2},{1,3},{2,0},{3,1},{4,6},{5,7},{6,4},{7,5},{8,10},{9,11},{10,... | collective-permute-start | bytes 393224 | tf_op jit(solution)/shard_map/ppermute | solution.py:542
  23.5 16.7 %collective-permute-start.6 = (f32[128,256]{1,0:T(8,128)S(1)}, f32[128,256]{1,0:T(8,128)S(1)}, u32[]{:S(2)}, u32[]{:S(2)}) collective-permute-start(f32[128,256]{1,0:T(8,128)S(1)} %get-tuple-element.68), channel_id=1, source_target_pairs={{0,4},{1,5},{2,6},{3,7},{4,0},{5,1},{6,2},{7,3},{8,12},{9,13},{10,... | collective-permute-start | bytes 393224 | tf_op jit(solution)/shard_map/ppermute | solution.py:542
  27.0 13.2 %collective-permute-start.7 = (f32[128,256]{1,0:T(8,128)S(1)}, f32[128,256]{1,0:T(8,128)S(1)}, u32[]{:S(2)}, u32[]{:S(2)}) collective-permute-start(f32[128,256]{1,0:T(8,128)S(1)} %get-tuple-element.69), channel_id=1, source_target_pairs={{0,6},{1,7},{2,4},{3,5},{4,2},{5,3},{6,0},{7,1},{8,14},{9,15},{10,... | collective-permute-start | bytes 393224 | tf_op jit(solution)/shard_map/ppermute | solution.py:542
  29.7 14.3 %collective-permute-start.11 = (f32[128,256]{1,0:T(8,128)S(1)}, f32[128,256]{1,0:T(8,128)S(1)}, u32[]{:S(2)}, u32[]{:S(2)}) collective-permute-start(f32[128,256]{1,0:T(8,128)S(1)} %get-tuple-element.60.refs_6_.refs_0_), channel_id=1, source_target_pairs={{0,8},{8,0},{16,24},{24,16},{1,9},{9,1},{17,25},{25,17},{2,10},{10... | collective-permute-start | bytes 393224 | tf_op jit(solution)/shard_map/ppermute | solution.py:549
  31.2 13.3 %collective-permute-start.12 = (f32[128,256]{1,0:T(8,128)S(1)}, f32[128,256]{1,0:T(8,128)S(1)}, u32[]{:S(2)}, u32[]{:S(2)}) collective-permute-start(f32[128,256]{1,0:T(8,128)S(1)} %get-tuple-element.60.refs_6_.refs_0_), channel_id=1, source_target_pairs={{0,16},{8,24},{16,0},{24,8},{1,17},{9,25},{17,1},{25,9},{2,18},{10... | collective-permute-start | bytes 393224 | tf_op jit(solution)/shard_map/ppermute | solution.py:549
  36.9 7.6 %collective-permute-start.13 = (f32[128,256]{1,0:T(8,128)S(1)}, f32[128,256]{1,0:T(8,128)S(1)}, u32[]{:S(2)}, u32[]{:S(2)}) collective-permute-start(f32[128,256]{1,0:T(8,128)S(1)} %get-tuple-element.60.refs_6_.refs_0_), channel_id=1, source_target_pairs={{0,24},{8,16},{16,8},{24,0},{1,25},{9,17},{17,9},{25,1},{2,26},{10... | collective-permute-start | bytes 393224 | tf_op jit(solution)/shard_map/ppermute | solution.py:549
  40.9 13.6 %collective-permute-start.10 = (f32[128,256]{1,0:T(8,128)S(1)}, f32[128,256]{1,0:T(8,128)S(1)}, u32[]{:S(2)}, u32[]{:S(2)}) collective-permute-start(f32[128,256]{1,0:T(8,128)S(1)} %get-tuple-element.71.refs_4_.refs_0_), channel_id=1, source_target_pairs={{0,24},{8,16},{16,8},{24,0},{1,25},{9,17},{17,9},{25,1},{2,26},{10... | collective-permute-start | bytes 393224 | tf_op jit(solution)/shard_map/ppermute | solution.py:549
  43.4 12.5 %collective-permute-start.8 = (f32[128,256]{1,0:T(8,128)S(1)}, f32[128,256]{1,0:T(8,128)S(1)}, u32[]{:S(2)}, u32[]{:S(2)}) collective-permute-start(f32[128,256]{1,0:T(8,128)S(1)} %get-tuple-element.71.refs_4_.refs_0_), channel_id=1, source_target_pairs={{0,8},{8,0},{16,24},{24,16},{1,9},{9,1},{17,25},{25,17},{2,10},{10... | collective-permute-start | bytes 393224 | tf_op jit(solution)/shard_map/ppermute | solution.py:549
  44.0 12.0 %collective-permute-start.9 = (f32[128,256]{1,0:T(8,128)S(1)}, f32[128,256]{1,0:T(8,128)S(1)}, u32[]{:S(2)}, u32[]{:S(2)}) collective-permute-start(f32[128,256]{1,0:T(8,128)S(1)} %get-tuple-element.71.refs_4_.refs_0_), channel_id=1, source_target_pairs={{0,16},{8,24},{16,0},{24,8},{1,17},{9,25},{17,1},{25,9},{2,18},{10... | collective-permute-start | bytes 393224 | tf_op jit(solution)/shard_map/ppermute | solution.py:549
  44.8 11.5 %collective-permute-start.17 = (f32[128,128]{1,0:T(8,128)S(1)}, f32[128,128]{1,0:T(8,128)S(1)}, u32[]{:S(2)}, u32[]{:S(2)}) collective-permute-start(f32[128,128]{1,0:T(8,128)S(1)} %get-tuple-element.80), channel_id=1, source_target_pairs={{0,2},{1,3},{2,0},{3,1},{4,6},{5,7},{6,4},{7,5},{8,10},{9,11},{10,... | collective-permute-start | bytes 196616 | tf_op jit(solution)/shard_map/ppermute | solution.py:564
  52.4 5.2 %collective-permute-start.18 = (f32[128,128]{1,0:T(8,128)S(1)}, f32[128,128]{1,0:T(8,128)S(1)}, u32[]{:S(2)}, u32[]{:S(2)}) collective-permute-start(f32[128,128]{1,0:T(8,128)S(1)} %get-tuple-element.81), channel_id=1, source_target_pairs={{0,4},{1,5},{2,6},{3,7},{4,0},{5,1},{6,2},{7,3},{8,12},{9,13},{10,... | collective-permute-start | bytes 196616 | tf_op jit(solution)/shard_map/ppermute | solution.py:564
  54.5 6.2 %collective-permute-start.19 = (f32[128,128]{1,0:T(8,128)S(1)}, f32[128,128]{1,0:T(8,128)S(1)}, u32[]{:S(2)}, u32[]{:S(2)}) collective-permute-start(f32[128,128]{1,0:T(8,128)S(1)} %get-tuple-element.82), channel_id=1, source_target_pairs={{0,6},{1,7},{2,4},{3,5},{4,2},{5,3},{6,0},{7,1},{8,14},{9,15},{10,... | collective-permute-start | bytes 196616 | tf_op jit(solution)/shard_map/ppermute | solution.py:564
  56.2 9.3 %copy-start.3 = (bf16[128,2048]{1,0:T(8,128)(2,1)S(1)}, bf16[128,2048]{1,0:T(8,128)(2,1)}, u32[]{:S(2)}) copy-start(bf16[128,2048]{1,0:T(8,128)(2,1)} %gate_ref.7) | copy-start | bytes 1572868
  61.0 6.2 %collective-permute-start.20 = (f32[4,128,128]{2,1,0:T(8,128)S(1)}, f32[4,128,128]{2,1,0:T(8,128)S(1)}, u32[]{:S(2)}, u32[]{:S(2)}) collective-permute-start(f32[4,128,128]{2,1,0:T(8,128)S(1)} %get-tuple-element.83), channel_id=1, source_target_pairs={{0,1},{1,0},{2,3},{3,2},{4,5},{5,4},{6,7},{7,6},{8,9},{9,8},{10,11... | collective-permute-start | bytes 786440 | tf_op jit(solution)/shard_map/ppermute | solution.py:568
  61.0 7.1 %collective-permute-start.14 = (f32[128,128]{1,0:T(8,128)S(1)}, f32[128,128]{1,0:T(8,128)S(1)}, u32[]{:S(2)}, u32[]{:S(2)}) collective-permute-start(f32[128,128]{1,0:T(8,128)S(1)} %get-tuple-element.75), channel_id=1, source_target_pairs={{0,2},{1,3},{2,0},{3,1},{4,6},{5,7},{6,4},{7,5},{8,10},{9,11},{10,... | collective-permute-start | bytes 196616 | tf_op jit(solution)/shard_map/ppermute | solution.py:564
  61.9 8.6 %collective-permute-start.15 = (f32[128,128]{1,0:T(8,128)S(1)}, f32[128,128]{1,0:T(8,128)S(1)}, u32[]{:S(2)}, u32[]{:S(2)}) collective-permute-start(f32[128,128]{1,0:T(8,128)S(1)} %get-tuple-element.76), channel_id=1, source_target_pairs={{0,4},{1,5},{2,6},{3,7},{4,0},{5,1},{6,2},{7,3},{8,12},{9,13},{10,... | collective-permute-start | bytes 196616 | tf_op jit(solution)/shard_map/ppermute | solution.py:564
  63.1 7.4 %collective-permute-start.16 = (f32[128,128]{1,0:T(8,128)S(1)}, f32[128,128]{1,0:T(8,128)S(1)}, u32[]{:S(2)}, u32[]{:S(2)}) collective-permute-start(f32[128,128]{1,0:T(8,128)S(1)} %get-tuple-element.77), channel_id=1, source_target_pairs={{0,6},{1,7},{2,4},{3,5},{4,2},{5,3},{6,0},{7,1},{8,14},{9,15},{10,... | collective-permute-start | bytes 196616 | tf_op jit(solution)/shard_map/ppermute | solution.py:564
  70.7 1.6 %collective-permute-start.21 = (f32[4,128,128]{2,1,0:T(8,128)S(1)}, f32[4,128,128]{2,1,0:T(8,128)S(1)}, u32[]{:S(2)}, u32[]{:S(2)}) collective-permute-start(f32[4,128,128]{2,1,0:T(8,128)S(1)} %get-tuple-element.86), channel_id=1, source_target_pairs={{0,1},{1,0},{2,3},{3,2},{4,5},{5,4},{6,7},{7,6},{8,9},{9,8},{10,11... | collective-permute-start | bytes 786440 | tf_op jit(solution)/shard_map/ppermute | solution.py:568
  (6 other events, 19.5 us)
